TPU v7x, 128 devices: a whole 4x4x4 slice. The times are simulated.
128 devices in a mesh: section: 4 (over z), space: 32 (over x, y, core).
Axes of the slice: x: 4, y: 4, z: 4, core: 2. Of those that a mesh axis runs over, the one named last changes fastest.
Arguments:
- features: bfloat16 [4, 128, 784, 256], P('section', 'space')
- tissue: int32 [4, 128], P('section'), may hold values from 0 to 1, as said below
- first_weight: bfloat16 [256, 512], replicated, may hold values from -0.375 to 0.375
- first_gain: float32 [512], replicated, may hold values from 0.1 to 1.9
- first_bias: float32 [512], replicated, may hold values from -3 to 3
- second_weight: bfloat16 [512, 1024], P(None, 'space'), may hold values from -0.25 to 0.25
- second_gain: float32 [1024], replicated, may hold values from 0.1 to 1.9
- second_bias: float32 [1024], replicated, may hold values from -3 to 3
Outputs:
- output: bfloat16 [4, 1024, 100352], P('section', 'space')
- first_mean: float32 [512], replicated
- first_var: float32 [512], replicated
- second_mean: float32 [1024], P('space')
- second_var: float32 [1024], P('space')
Inputs may be any that keep to these rules, and one draw needn't show every extreme that they name: Every tile row holds at least one tissue tile and at least one tile without tissue.
All inputs are finite; a program needn't handle non-finite values.
Results may differ from a plain program's by a relative error of at most 0.0053.
Values may be sent and summed in bfloat16 or wider, within the bound.
No kernel may reach another device: no remote copies, remote signals or barrier semaphores. Data moves between devices by JAX's collectives and lax.ppermute only.
A program may use at most 128 MiB of HBM per device.

v0:
```python
import jax
import jax.numpy as jnp
from jax import lax
from jax.experimental import pallas as pl
from jax.experimental.pallas import tpu as pltpu
from jax.sharding import Mesh
from jax.sharding import PartitionSpec as P


EPS = 1e-05
EVERY = ("z", "x", "y", "c")
PLANE = ("x", "y", "c")
RING = 4
BAND = 128
HALF = BAND // 2
PIECE = 512


def place(x, y, c):
    return ((x % RING) * RING + y % RING) * 2 + c


def along(step, core0_axis, flip):
    pairs = []
    for x in range(RING):
        for y in range(RING):
            for c in range(2):
                on_x = (core0_axis == "x") == (c == 0)
                there = (x + step, y) if on_x else (x, y + step)
                pairs.append((place(x, y, c), place(*there, c ^ flip)))
    return pairs


def gather_step(values, step):
    return lax.ppermute(values, PLANE, along(step, "x", 0))


def exchange_step(values, step, flip):
    return lax.ppermute(values, PLANE, along(step, "y", flip))


def spot():
    return tuple(lax.axis_index(axis) for axis in PLANE)


def tissue_of(tissue_ref, chip_x, chip_y, core, tiles):
    base = place(chip_x, chip_y, core) * tiles
    return [tissue_ref[base + t].astype(jnp.float32) for t in range(tiles)]


def ring_spot(slot):
    x, y, c = spot()
    along_x, along_y = (1 - c) * slot, c * slot
    return (x + RING - along_x) % RING, (y + RING - along_y) % RING, c


def merge(counts, means, squares):
    total = jnp.sum(counts, axis=0)
    centre = means[0]
    mean_val = centre + jnp.sum(counts * (means - centre), axis=0) / jnp.maximum(total, 1.0)
    spread = jnp.sum(squares + counts * (means - mean_val) ** 2, axis=0)
    return total, mean_val, spread


def local_moments(count, centre, sums, squares):
    safe = jnp.maximum(count, 1.0)
    return centre + sums / safe, squares - sums * sums / safe


def first_kernel(tissue_ref, rows_ref, weight_ref, own_ref, mate_ref, out_ref, turned_ref, pair_ref, acc_ref):
    step = pl.program_id(0)
    tiles = pl.num_programs(0)
    pixels = rows_ref.shape[0]
    base = place(*spot()) * tiles
    first = jnp.dot(rows_ref[...], weight_ref[...], preferred_element_type=jnp.float32)

    @pl.when(step == 0)
    def _():
        acc_ref[...] = jnp.zeros_like(acc_ref)
        acc_ref[0:1, :] = jnp.mean(first, axis=0, keepdims=True)
        turned_ref[...] = weight_ref[...].T
        width = own_ref.shape[0]
        pair_ref[:width, :] = own_ref[...]
        pair_ref[width:, :] = mate_ref[...]

    centred = first - acc_ref[0:1, :]
    held = tissue_ref[base + step].astype(jnp.float32)
    acc_ref[1:2, :] += held * jnp.sum(centred, axis=0, keepdims=True)
    acc_ref[2:3, :] += held * jnp.sum(centred * centred, axis=0, keepdims=True)
    acc_ref[3:4, :] += jnp.full((1, acc_ref.shape[1]), held * pixels, jnp.float32)

    @pl.when(step == tiles - 1)
    def _():
        count = acc_ref[3:4, :]
        mean, spread = local_moments(count, acc_ref[0:1, :], acc_ref[1:2, :], acc_ref[2:3, :])
        parts = acc_ref.shape[1] // BAND
        for r, row in enumerate((count, mean, spread)):
            for q in range(parts):
                out_ref[:, r * parts + q, :] = jnp.broadcast_to(
                    row[:, q * BAND : (q + 1) * BAND], (out_ref.shape[0], BAND)
                )


def first_sums(tissue, rows, weight, own, mate, members):
    tiles, pixels, depth = rows.shape
    width = weight.shape[1]
    whole = lambda shape: pl.BlockSpec(shape, lambda i, t: (0,) * len(shape))
    return pl.pallas_call(
        first_kernel,
        out_shape=[
            jax.ShapeDtypeStruct((members, 16, BAND), jnp.float32),
            jax.ShapeDtypeStruct((width, depth), jnp.bfloat16),
            jax.ShapeDtypeStruct((2 * own.shape[0], own.shape[1]), jnp.bfloat16),
        ],
        grid_spec=pltpu.PrefetchScalarGridSpec(
            num_scalar_prefetch=1,
            grid=(tiles,),
            in_specs=[
                pl.BlockSpec((None, pixels, depth), lambda i, t: (i, 0, 0)),
                whole(weight.shape),
                whole(own.shape),
                whole(mate.shape),
            ],
            out_specs=[
                whole((members, 16, BAND)),
                whole((width, depth)),
                whole((2 * own.shape[0], own.shape[1])),
            ],
            scratch_shapes=[pltpu.VMEM((8, width), jnp.float32)],
        ),
        compiler_params=pltpu.CompilerParams(dimension_semantics=("arbitrary",)),
        name="first_sums",
    )(tissue, rows, weight, own, mate)


def near_merge_kernel(in_ref, out_ref):
    parts = 4
    got = in_ref[...]
    rows = merge(*(got[:, r * parts : (r + 1) * parts, :] for r in range(3)))
    for r, row in enumerate(rows):
        out_ref[:, r * parts : (r + 1) * parts, :] = jnp.broadcast_to(
            row[None], (out_ref.shape[0], parts, BAND)
        )


def near_merge(messages, members):
    return pl.pallas_call(
        near_merge_kernel,
        out_shape=jax.ShapeDtypeStruct((members, 16, BAND), jnp.float32),
        name="near_merge",
    )(messages)


def whole_merge_kernel(in_ref, gain_ref, bias_ref, mean_ref, var_ref, mean_col, scale_col, bias_col):
    parts = mean_ref.shape[0]
    got = in_ref[...]
    count, mean, spread = merge(*(got[:, r * parts : (r + 1) * parts, :] for r in range(3)))
    var = spread / count
    mean_ref[...] = mean
    var_ref[...] = var
    for value, col in (
        (mean, mean_col),
        (gain_ref[...] * lax.rsqrt(var + EPS), scale_col),
        (bias_ref[...], bias_col),
    ):
        for q in range(parts):
            col[q * BAND : (q + 1) * BAND, :] = jnp.broadcast_to(value[q : q + 1, :], (BAND, BAND)).T


def whole_merge(messages, gain, bias):
    width = gain.shape[0]
    row = jax.ShapeDtypeStruct((width // BAND, BAND), jnp.float32)
    col = jax.ShapeDtypeStruct((width, BAND), jnp.float32)
    return pl.pallas_call(
        whole_merge_kernel, out_shape=[row, row, col, col, col], name="whole_merge"
    )(messages, gain.reshape(row.shape), bias.reshape(row.shape))


def make_second_kernel(cuts, order, pixels, tiles, lanes, last):
    n_in = sum(len(c) for c in cuts)
    slots = len(cuts)

    def kernel(tissue_ref, *refs):
        inputs = refs[:n_in]
        w1_ref, mean_ref, scale_ref, bias_ref = refs[n_in : n_in + 4]
        w2_refs = refs[n_in + 4 : n_in + 8]
        rest = refs[n_in + 8 :]
        if last:
            before_ref, rest = rest[0], rest[1:]
        outs, stats_ref, rows, w2_ref, sems = rest[:8], rest[8], rest[9], rest[10], rest[11]
        core = lax.axis_index("c")
        shift = pl.multiple_of(core * HALF, HALF)

        def copies(slot):
            first_input = sum(len(c) for c in cuts[:slot])
            return [
                pltpu.make_async_copy(
                    inputs[first_input + i],
                    rows.at[slot, pl.ds(pl.multiple_of(shift + start, 16), size), :],
                    sems.at[first_input + i],
                )
                for i, (start, size) in enumerate(cuts[slot])
            ]

        for slot in range(slots):
            for copy in copies(slot):
                copy.start()
            rest_at = pl.multiple_of((1 - core) * (lanes - HALF), HALF)
            rows[slot, pl.ds(rest_at, HALF), :] = jnp.zeros((HALF, rows.shape[2]), rows.dtype)
        for i, ref in enumerate(w2_refs):
            w2_ref[i * ref.shape[0] : (i + 1) * ref.shape[0], :] = ref[...]
        width = outs[0].shape[1]
        centre = jnp.broadcast_to(before_ref[:, 0:1], (8 * width, BAND)) if last else None
        sums = squares = None
        for slot in range(slots):
            held_here = tissue_of(tissue_ref, *ring_spot(order[slot]), tiles)
            for copy in copies(slot):
                copy.wait()
            for at in range(0, lanes, PIECE):
                tile = min(PIECE, lanes - at)
                wide = lambda v: jnp.concatenate([v] * (tile // BAND), axis=1)
                block = rows[slot, at : at + tile, :]
                first = lax.dot_general(
                    w1_ref[...],
                    block,
                    (((1,), (1,)), ((), ())),
                    preferred_element_type=jnp.float32,
                )
                activation = jnp.maximum(
                    (first - wide(mean_ref[...])) * wide(scale_ref[...]) + wide(bias_ref[...]), 0.0
                ).astype(jnp.bfloat16)
                second = jnp.dot(w2_ref[...], activation, preferred_element_type=jnp.float32)
                if centre is None:
                    centre = jnp.broadcast_to(
                        jnp.mean(second[:, BAND:], axis=1, keepdims=True), (8 * width, BAND)
                    )
                second = second - wide(centre)
                lane = lax.broadcasted_iota(jnp.int32, (1, tile), 1) + (at - shift)
                held = jnp.zeros((1, tile), jnp.float32)
                for t in range(tiles):
                    inside = (lane >= t * pixels) & (lane < (t + 1) * pixels)
                    held += jnp.where(inside, held_here[t], 0.0)
                kept = second * held
                squared = kept * second
                part = sum(kept[:, i * BAND : (i + 1) * BAND] for i in range(tile // BAND))
                part2 = sum(squared[:, i * BAND : (i + 1) * BAND] for i in range(tile // BAND))
                sums = part if sums is None else sums + part
                squares = part2 if squares is None else squares + part2
                rounded = second.astype(jnp.bfloat16)
                for i in range(8):
                    outs[i][slot, :, at : at + tile] = rounded[i * width : (i + 1) * width, :]
        lane = lax.broadcasted_iota(jnp.int32, (8 * width, BAND), 1)
        sums = jnp.sum(sums, axis=1, keepdims=True)
        squares = jnp.sum(squares, axis=1, keepdims=True)
        if last:
            count = sum(
                held for slot in range(RING) for held in tissue_of(tissue_ref, *ring_spot(slot), tiles)
            )
            count = jnp.full((8 * width, 1), count * pixels, jnp.float32)
            mean, spread = local_moments(
                count, before_ref[:, 0:1], before_ref[:, 1:2] + sums, before_ref[:, 2:3] + squares
            )
            message = jnp.where(lane == 0, count, jnp.where(lane == 1, mean, spread)).T[:8, :]
            stats_ref[...] = jnp.broadcast_to(message[None], stats_ref.shape)
        else:
            stats_ref[...] = jnp.where(lane == 0, centre, jnp.where(lane == 1, sums, squares))

    return kernel


def second_values(tissue, groups, order, norm, pairs, before, pixels, tiles):
    cuts, inputs = [], []
    for blocks in groups:
        start, cut = 0, []
        for block in blocks:
            cut.append((start, block.shape[0]))
            inputs.append(block)
            start += block.shape[0]
        cuts.append(tuple(cut))
    depth = norm[0].shape[1]
    lanes = pixels * tiles + HALF
    channels = sum(pair.shape[0] for pair in pairs)
    vmem = pl.BlockSpec(memory_space=pltpu.VMEM)
    extra = [] if before is None else [before]
    stats = (channels, BAND) if before is None else (RING, 8, channels)
    outs = pl.pallas_call(
        make_second_kernel(tuple(cuts), order, pixels, tiles, lanes, before is not None),
        out_shape=[jax.ShapeDtypeStruct((len(groups), channels // 8, lanes), jnp.bfloat16)] * 8
        + [jax.ShapeDtypeStruct(stats, jnp.float32)],
        in_specs=[pl.BlockSpec(memory_space=pltpu.SMEM)]
        + [pl.BlockSpec(memory_space=pl.ANY)] * len(inputs)
        + [vmem] * (8 + len(extra)),
        out_specs=[vmem] * 9,
        scratch_shapes=[
            pltpu.VMEM((len(groups), lanes, depth), jnp.bfloat16),
            pltpu.VMEM((channels, norm[0].shape[0]), jnp.bfloat16),
            pltpu.SemaphoreType.DMA((len(inputs),)),
        ],
        name="second_values",
    )(tissue, *inputs, *norm, *pairs, *extra)
    return outs[:8], outs[8]


def letters_kernel(in_ref, before_ref, *outs):
    got = in_ref[...]
    channels = got.shape[2]
    rows = merge(got[:, 0:1, :], got[:, 1:2, :], got[:, 2:3, :])
    stacked = jnp.concatenate([*rows, jnp.zeros((BAND - 3, channels), jnp.float32)], axis=0).T
    lane = lax.broadcasted_iota(jnp.int32, stacked.shape, 1)
    stacked = jnp.where(lane == 3, before_ref[:, 0:1], stacked)
    width = channels // 8
    for i, out in enumerate(outs):
        out[...] = stacked[i * width : (i + 1) * width, :]


def letters_of(messages, before):
    width = before.shape[0] // 8
    return pl.pallas_call(
        letters_kernel,
        out_shape=[jax.ShapeDtypeStruct((width, BAND), jnp.float32)] * 8,
        name="letters",
    )(messages, before)


def make_last_kernel(chip_lanes):
    cut = chip_lanes // 2 // BAND * BAND

    def kernel(*refs):
        moved, letters = refs[:16], refs[16:24]
        gain_ref, bias_ref, out_ref, mean_ref, var_ref = refs[24:29]
        inbuf, outbuf, offset_ref, in_sems, out_sems = refs[29:]
        x, y, core = spot()

        def piece(ring, slot, flip):
            group, row = ((0, 0), (0, 1), (1, 0), (0, 2))[slot]
            return moved[group * 8 + ring * 2 + flip].at[row]

        def loads(a, b, c):
            n = a * RING + b
            return (
                pltpu.make_async_copy(piece(b, a, c), inbuf.at[n, 0], in_sems.at[n, 0]),
                pltpu.make_async_copy(piece(a, b, 1 - c), inbuf.at[n, 1], in_sems.at[n, 1]),
            )

        def store(a, b):
            n = a * RING + b
            chip = ((x + RING - a) % RING) * RING + (y + RING - b) % RING
            return pltpu.make_async_copy(
                outbuf.at[n],
                out_ref.at[:, pl.ds(pl.multiple_of(chip * chip_lanes, BAND), chip_lanes)],
                out_sems.at[n],
            )

        steps = [(a, b) for a in range(RING) for b in range(RING)]
        for a, b in steps:
            for c in range(2):

                @pl.when(core == c)
                def _():
                    for copy in loads(a, b, c):
                        copy.start()

        width = letters[0].shape[0]
        got = jnp.stack([ref[...] for ref in letters])
        count, mean, spread = merge(got[:, :, 0:1], got[:, :, 1:2], got[:, :, 2:3])
        var = spread / count
        for i in range(8):
            offset_ref[i] = jnp.broadcast_to(got[i, :, 3:4] - mean, (width, BAND))
        lane = lax.broadcasted_iota(jnp.int32, (width, BAND), 1)
        row = lax.broadcasted_iota(jnp.int32, (width, BAND), 0)
        device = place(x, y, core)
        per_row = BAND // width

        def own_channels(ref):
            line = ref[pl.ds(device // per_row, 1), :]
            here = lane == row + (device % per_row) * width
            return jnp.sum(jnp.where(here, line, 0.0), axis=1, keepdims=True)

        scale = jnp.broadcast_to(own_channels(gain_ref) * lax.rsqrt(var + EPS), (width, BAND))
        bias = jnp.broadcast_to(own_channels(bias_ref), (width, BAND))
        for value, ref in ((mean, mean_ref), (var, var_ref)):
            line = jnp.sum(jnp.where(lane == row, value, 0.0), axis=0, keepdims=True)
            ref[...] = line[:, :width]

        def finish(values, offset):
            wide = lambda v: jnp.concatenate([v] * (values.shape[1] // BAND), axis=1)
            return jnp.maximum(
                (values.astype(jnp.float32) + wide(offset)) * wide(scale) + wide(bias), 0.0
            )

        for a, b in steps:
            n = a * RING + b
            for c in range(2):

                @pl.when(core == c)
                def _():
                    for copy in loads(a, b, c):
                        copy.wait()

            left_offset = offset_ref[b * 2 + core]
            right_offset = offset_ref[a * 2 + 1 - core]
            left = inbuf.at[n, 0]
            right = inbuf.at[n, 1]
            outbuf[n, :, :cut] = finish(left[:, :cut], left_offset).astype(jnp.bfloat16)
            middle = jnp.where(
                lane < HALF,
                finish(left[:, cut : cut + BAND], left_offset),
                finish(right[:, :BAND], right_offset),
            )
            outbuf[n, :, cut : cut + BAND] = middle.astype(jnp.bfloat16)
            outbuf[n, :, cut + BAND :] = finish(right[:, BAND:], right_offset).astype(jnp.bfloat16)
            store(a, b).start()
        for a, b in steps:
            store(a, b).wait()

    return kernel


def last_pass(moved, letters, gain, bias, chip_lanes):
    _, width, lanes = moved[0].shape
    vmem = pl.BlockSpec(memory_space=pltpu.VMEM)
    hbm = pl.BlockSpec(memory_space=pl.ANY)
    chips = RING * RING
    stat = jax.ShapeDtypeStruct((1, width), jnp.float32)
    return pl.pallas_call(
        make_last_kernel(chip_lanes),
        out_shape=[jax.ShapeDtypeStruct((width, chips * chip_lanes), jnp.bfloat16), stat, stat],
        in_specs=[hbm] * 16 + [vmem] * 10,
        out_specs=[hbm, vmem, vmem],
        scratch_shapes=[
            pltpu.VMEM((chips, 2, width, lanes), jnp.bfloat16),
            pltpu.VMEM((chips, width, chip_lanes), jnp.bfloat16),
            pltpu.VMEM((8, width, BAND), jnp.float32),
            pltpu.SemaphoreType.DMA((chips, 2)),
            pltpu.SemaphoreType.DMA((chips,)),
        ],
        name="last_pass",
    )(*moved, *letters, gain.reshape(-1, BAND), bias.reshape(-1, BAND))


def trade(messages, axes):
    return lax.all_to_all(messages, axes, split_axis=0, concat_axis=0, tiled=True)


ROUTES = [(step, flip) for step in range(RING) for flip in range(2)]


def send(blocks):
    return [
        block if route == (0, 0) else exchange_step(block, *route)
        for route, block in zip(ROUTES, blocks)
    ]


def shards(
    features, tissue, first_weight, first_gain, first_bias, second_weight, second_gain, second_bias
):
    tiles, pixels, depth = features.shape[1:]
    rows = features.reshape(tiles * pixels, depth)
    row_tissue = tissue[0]
    half = tiles * pixels // 2
    own = second_weight.T
    mate = lax.ppermute(own, "c", [(0, 1), (1, 0)])
    ahead = gather_step(rows, 1)
    behind = gather_step(rows, 3)
    messages, w1t, pair = first_sums(
        row_tissue, features[0], first_weight, own, mate, 2 * RING
    )
    pairs = [pair] + [exchange_step(pair, step, 0) for step in (3, 2, 1)]
    messages = trade(messages, ("z", "c"))
    messages, pairs = lax.optimization_barrier((messages, pairs))
    messages = near_merge(messages, RING * RING)
    messages = trade(messages, ("x", "y"))
    far = [gather_step(ahead[:half], 1), gather_step(behind[half:], 3)]
    first_mean, first_var, *norm = whole_merge(messages, first_gain, first_bias)
    near, before = second_values(
        row_tissue, [[rows], [ahead], [behind]], (0, 1, 3), (w1t, *norm), pairs, None, pixels, tiles
    )
    moved = send(near)
    rest, messages = second_values(
        row_tissue, [far], (2,), (w1t, *norm), pairs, before, pixels, tiles
    )
    moved += send(rest)
    messages = trade(messages, ("z",))
    letters = letters_of(messages, before)
    letters = send(letters)
    output, second_mean, second_var = last_pass(
        moved, letters, second_gain, second_bias, 2 * tiles * pixels
    )
    return (
        output[None],
        first_mean.reshape(-1),
        first_var.reshape(-1),
        second_mean[0],
        second_var[0],
    )


def solution(mesh):
    fine = Mesh(mesh.devices.reshape(RING, RING, RING, 2), EVERY)
    in_specs = (
        P("z", PLANE, None, None),
        P("z", None),
        P(),
        P(),
        P(),
        P(None, PLANE),
        P(),
        P(),
    )
    out_specs = (P("z", PLANE, None), P(), P(), P(PLANE), P(PLANE))
    return jax.shard_map(
        shards, mesh=fine, in_specs=in_specs, out_specs=out_specs, check_vma=False
    )
```

profile of v0, /device:TPU:1, one launch (start us, length us, event | category | flops | bytes accessed | tf_op | source)
XLA Modules:
  0.0 135.1 jit_solution(9670635513049214505)
XLA Ops:
  0.6 3.6 %collective-permute-start.1 = (bf16[3136,256]{1,0:T(8,128)(2,1)}, bf16[3136,256]{1,0:T(8,128)(2,1)S(1)}, u32[]{:S(2)}, u32[]{:S(2)}) collective-permute-start(bf16[3136,256]{1,0:T(8,128)(2,1)} %bitcast.13), channel_id=1, source_target_pairs={{0,24},{1,7},{2,26},{3,1},{4,28},{5,3},{6,30},{7,5},{8,0},{9,15},{... | collective-permute-start | bytes 4816904 | tf_op jit(solution)/shard_map/ppermute | solution.py:35
  6.6 5.6 %first_sums.1 = (f32[8,16,128]{2,1,0:T(8,128)}, bf16[512,256]{1,0:T(8,128)(2,1)}, bf16[64,512]{1,0:T(8,128)(2,1)}) custom-call(s32[128]{0:T(128)} %bitcast.19, bf16[4,784,256]{2,1,0:T(8,128)(2,1)} %bitcast.15, bf16[256,512]{1,0:T(8,128)(2,1)} %weight_ref.1, bf16[32,512]{1,0:T(8,128)(2,1)} %bitcast.18, bf16[32,512]{1,0:T(8,128)(2,1)} %copy-done.18), custom_call_target="tpu_custom_call" | custom-call | tf_op jit(solution)/shard_map/first_sums/pallas_call | solution.py:108
  13.1 3.3 %collective-permute-start.4 = (bf16[64,512]{1,0:T(8,128)(2,1)}, bf16[64,512]{1,0:T(8,128)(2,1)S(1)}, u32[]{:S(2)}, u32[]{:S(2)}) collective-permute-start(bf16[64,512]{1,0:T(8,128)(2,1)} %get-tuple-element.54.refs_7_.refs_6_), channel_id=1, source_target_pairs={{0,4},{1,17},{2,6},{3,19},{4,0},{5,21},{6,2},{7,23},{8,12},{9,25},... | collective-permute-start | bytes 196616 | tf_op jit(solution)/shard_map/ppermute | solution.py:39
  16.7 12.0 %all_to_all.15.in_ref = f32[8,16,128]{2,1,0:T(8,128)} all-to-all(f32[8,16,128]{2,1,0:T(8,128)} %get-tuple-element.48), channel_id=1, replica_groups=mesh['z'=4,'x'=4,'y'=4,'c'=2] {'z','c'}, dimensions={0} | all-to-all | bytes 131072 | tf_op jit(solution)/shard_map/all_to_all | solution.py:442
  30.3 4.4 %all-to-all-start.1 = ((f32[16,16,128]{2,1,0:T(8,128)}), f32[16,16,128]{2,1,0:T(8,128)S(1)}, u32[]{:S(2)}, u32[]{:S(2)}) async-start(f32[16,16,128]{2,1,0:T(8,128)} %near_merge.1), calls=%async_computation.1 | async-start | bytes 262144 | tf_op jit(solution)/shard_map/all_to_all | solution.py:442
  35.8 2.6 %collective-permute-start.14 = (bf16[1568,256]{1,0:T(8,128)(2,1)}, bf16[1568,256]{1,0:T(8,128)(2,1)}, u32[]{:S(2)}, u32[]{:S(2)}) collective-permute-start(bf16[1568,256]{1,0:T(8,128)(2,1)} %slice.9), channel_id=1, source_target_pairs={{0,24},{1,7},{2,26},{3,1},{4,28},{5,3},{6,30},{7,5},{8,0},{9,15},{... | collective-permute-start | bytes 2408456 | tf_op jit(solution)/shard_map/ppermute | solution.py:35
  39.7 1.8 %all-to-all-done.1.in_ref = f32[16,16,128]{2,1,0:T(8,128)S(1)} async-done(((f32[16,16,128]{2,1,0:T(8,128)}), f32[16,16,128]{2,1,0:T(8,128)S(1)}, u32[]{:S(2)}, u32[]{:S(2)}) %all-to-all-start.1) | async-done | bytes 131104 | tf_op jit(solution)/shard_map/all_to_all | solution.py:442
  42.2 2.0 %whole_merge.1 = (f32[4,128]{1,0:T(4,128)}, f32[4,128]{1,0:T(4,128)}, f32[512,128]{1,0:T(8,128)}, f32[512,128]{1,0:T(8,128)}, f32[512,128]{1,0:T(8,128)}) custom-call(f32[16,16,128]{2,1,0:T(8,128)} %copy-done.7, f32[4,128]{1,0:T(4,128)} %bitcast.24, f32[4,128]{1,0:T(4,128)} %bitcast.25), custom_call_target="tpu_custom_call" | custom-call | tf_op jit(solution)/shard_map/whole_merge/pallas_call | solution.py:174
  44.1 13.8 %second_values.2 = (bf16[3,32,3200]{2,1,0:T(8,128)(2,1)}, bf16[3,32,3200]{2,1,0:T(8,128)(2,1)}, bf16[3,32,3200]{2,1,0:T(8,128)(2,1)}, bf16[3,32,3200]{2,1,0:T(8,...) custom-call(s32[128]{0:T(128)} %bitcast.20, ...), custom_call_target="tpu_custom_call" | custom-call | tf_op jit(solution)/shard_map/second_values/pallas_call | solution.py:286
  58.0 2.3 %collective-permute-start.6 = (bf16[3,32,3200]{2,1,0:T(8,128)(2,1)}, bf16[3,32,3200]{2,1,0:T(8,128)(2,1)S(1)}, u32[]{:S(2)}, u32[]{:S(2)}) collective-permute-start(bf16[3,32,3200]{2,1,0:T(8,128)(2,1)} %get-tuple-element.59), channel_id=1, source_target_pairs={{0,1},{1,0},{2,3},{3,2},{4,5},{5,4},{6,7},{7,6},{8,9},{9,8},{10,11... | collective-permute-start | bytes 1843208 | tf_op jit(solution)/shard_map/ppermute | solution.py:39
  63.4 7.5 %collective-permute-done.7.refs_2_ = bf16[3,32,3200]{2,1,0:T(8,128)(2,1)S(1)} collective-permute-done((bf16[3,32,3200]{2,1,0:T(8,128)(2,1)}, bf16[3,32,3200]{2,1,0:T(8,128)(2,1)S(1)}, u32[]{:S(2)}, u32[]{:S(2)}) %collective-permute-start.7) | collective-permute-done | bytes 614432 | tf_op jit(solution)/shard_map/ppermute | solution.py:39
  70.9 1.8 %collective-permute-start.10 = (bf16[3,32,3200]{2,1,0:T(8,128)(2,1)}, bf16[3,32,3200]{2,1,0:T(8,128)(2,1)S(1)}, u32[]{:S(2)}, u32[]{:S(2)}) collective-permute-start(bf16[3,32,3200]{2,1,0:T(8,128)(2,1)} %get-tuple-element.63), channel_id=1, source_target_pairs={{0,5},{1,16},{2,7},{3,18},{4,1},{5,20},{6,3},{7,22},{8,13},{9,24},... | collective-permute-start | bytes 1843208 | tf_op jit(solution)/shard_map/ppermute | solution.py:39
  74.5 6.7 %second_values.3 = (bf16[1,32,3200]{2,1,0:T(8,128)(2,1)}, bf16[1,32,3200]{2,1,0:T(8,128)(2,1)}, bf16[1,32,3200]{2,1,0:T(8,128)(2,1)}, bf16[1,32,3200]{2,1,0:T(8,...) custom-call(s32[128]{0:T(128)} %bitcast.21, ...), custom_call_target="tpu_custom_call" | custom-call | tf_op jit(solution)/shard_map/second_values/pallas_call | solution.py:286
  81.2 9.7 %collective-permute-done.8.refs_3_ = bf16[3,32,3200]{2,1,0:T(8,128)(2,1)S(1)} collective-permute-done((bf16[3,32,3200]{2,1,0:T(8,128)(2,1)}, bf16[3,32,3200]{2,1,0:T(8,128)(2,1)S(1)}, u32[]{:S(2)}, u32[]{:S(2)}) %collective-permute-start.8) | collective-permute-done | bytes 614432 | tf_op jit(solution)/shard_map/ppermute | solution.py:39
  91.2 8.2 %all_to_all.16.in_ref = f32[4,8,256]{2,1,0:T(8,128)} all-to-all(f32[4,8,256]{2,1,0:T(8,128)} %get-tuple-element.75), channel_id=1, replica_groups=mesh['z'=4,'x'=4,'y'=4,'c'=2] {'z'}, dimensions={0} | all-to-all | bytes 65536 | tf_op jit(solution)/shard_map/all_to_all | solution.py:442
  99.4 1.8 %letters.1 = (f32[32,128]{1,0:T(8,128)}, f32[32,128]{1,0:T(8,128)}, f32[32,128]{1,0:T(8,128)}, f32[32,128]{1,0:T(8,128)}, f32[32,128]{1,0:T(8,128)}, /*index=5*/...) custom-call(f32[4,8,256]{2,1,0:T(8,128)} %all_to_all.16.in_ref, f32[256,128]{1,0:T(8,128)} %get-tuple-element.66.refs_10_.before_ref), custom_call_target="tpu_custom_call" | custom-call | tf_op jit(solution)/shard_map/letters/pallas_call | solution.py:318
  103.8 1.8 %collective-permute-start.25 = (f32[32,128]{1,0:T(8,128)}, f32[32,128]{1,0:T(8,128)S(1)}, u32[]{:S(2)}, u32[]{:S(2)}) collective-permute-start(f32[32,128]{1,0:T(8,128)} %get-tuple-element.80), channel_id=1, source_target_pairs={{0,4},{1,17},{2,6},{3,19},{4,0},{5,21},{6,2},{7,23},{8,12},{9,25},... | collective-permute-start | bytes 49160 | tf_op jit(solution)/shard_map/ppermute | solution.py:39
  106.7 2.1 %collective-permute-start.26 = (f32[32,128]{1,0:T(8,128)}, f32[32,128]{1,0:T(8,128)S(1)}, u32[]{:S(2)}, u32[]{:S(2)}) collective-permute-start(f32[32,128]{1,0:T(8,128)} %get-tuple-element.81), channel_id=1, source_target_pairs={{0,5},{1,16},{2,7},{3,18},{4,1},{5,20},{6,3},{7,22},{8,13},{9,24},... | collective-permute-start | bytes 49160 | tf_op jit(solution)/shard_map/ppermute | solution.py:39
  113.0 3.2 %collective-permute-start.18 = (bf16[1,32,3200]{2,1,0:T(8,128)(2,1)}, bf16[1,32,3200]{2,1,0:T(8,128)(2,1)S(1)}, u32[]{:S(2)}, u32[]{:S(2)}) collective-permute-start(bf16[1,32,3200]{2,1,0:T(8,128)(2,1)} %get-tuple-element.71), channel_id=1, source_target_pairs={{0,4},{1,17},{2,6},{3,19},{4,0},{5,21},{6,2},{7,23},{8,12},{9,25},... | collective-permute-start | bytes 614408 | tf_op jit(solution)/shard_map/ppermute | solution.py:39
  116.3 1.7 %collective-permute-start.20 = (bf16[1,32,3200]{2,1,0:T(8,128)(2,1)}, bf16[1,32,3200]{2,1,0:T(8,128)(2,1)S(1)}, u32[]{:S(2)}, u32[]{:S(2)}) collective-permute-start(bf16[1,32,3200]{2,1,0:T(8,128)(2,1)} %get-tuple-element.73), channel_id=1, source_target_pairs={{0,6},{1,25},{2,0},{3,27},{4,2},{5,29},{6,4},{7,31},{8,14},{9,1},{... | collective-permute-start | bytes 614408 | tf_op jit(solution)/shard_map/ppermute | solution.py:39
  119.6 2.5 %collective-permute-done.18.refs_12_ = bf16[1,32,3200]{2,1,0:T(8,128)(2,1)S(1)} collective-permute-done((bf16[1,32,3200]{2,1,0:T(8,128)(2,1)}, bf16[1,32,3200]{2,1,0:T(8,128)(2,1)S(1)}, u32[]{:S(2)}, u32[]{:S(2)}) %collective-permute-start.18) | collective-permute-done | bytes 204832 | tf_op jit(solution)/shard_map/ppermute | solution.py:39
  122.0 2.2 %collective-permute-done.19.refs_13_ = bf16[1,32,3200]{2,1,0:T(8,128)(2,1)S(1)} collective-permute-done((bf16[1,32,3200]{2,1,0:T(8,128)(2,1)}, bf16[1,32,3200]{2,1,0:T(8,128)(2,1)S(1)}, u32[]{:S(2)}, u32[]{:S(2)}) %collective-permute-start.19) | collective-permute-done | bytes 204832 | tf_op jit(solution)/shard_map/ppermute | solution.py:39
  124.2 2.5 %collective-permute-done.21.refs_15_ = bf16[1,32,3200]{2,1,0:T(8,128)(2,1)S(1)} collective-permute-done((bf16[1,32,3200]{2,1,0:T(8,128)(2,1)}, bf16[1,32,3200]{2,1,0:T(8,128)(2,1)S(1)}, u32[]{:S(2)}, u32[]{:S(2)}) %collective-permute-start.21) | collective-permute-done | bytes 204832 | tf_op jit(solution)/shard_map/ppermute | solution.py:39
  127.4 7.5 %last_pass.1 = (bf16[32,100352]{1,0:T(8,128)(2,1)}, f32[1,32]{1,0:T(1,128)}, f32[1,32]{1,0:T(1,128)}) custom-call(bf16[3,32,3200]{2,1,0:T(8,128)(2,1)} %get-tuple-element.58.refs_0_, bf16[3,32,3200]{2,1,0:T(8,128)(2,1)} %copy-done.2, bf16[3,32,3200]{2,1,0:T(8,128)(2,1)} %copy-done.3, bf16[3,32,3200]{2,1,0:T(8,128)(2,1)} %copy-done.4, ...), custom_call_target="tpu_custom_call" | custom-call | tf_op jit(solution)/shard_map/last_pass/pallas_call | solution.py:425
  (99 shorter events, 23.5 us)
Async XLA Ops:
  0.6 34.1 %collective-permute-start.1 = (bf16[3136,256]{1,0:T(8,128)(2,1)}, bf16[3136,256]{1,0:T(8,128)(2,1)S(1)}, u32[]{:S(2)}, u32[]{:S(2)}) collective-permute-start(bf16[3136,256]{1,0:T(8,128)(2,1)} %bitcast.13), channel_id=1, source_target_pairs={{0,24},{1,7},{2,26},{3,1},{4,28},{5,3},{6,30},{7,5},{8,0},{9,15},{... | collective-permute-start | bytes 4816904 | tf_op jit(solution)/shard_map/ppermute | solution.py:35
  4.3 34.1 %collective-permute-start = (bf16[3136,256]{1,0:T(8,128)(2,1)}, bf16[3136,256]{1,0:T(8,128)(2,1)S(1)}, u32[]{:S(2)}, u32[]{:S(2)}) collective-permute-start(bf16[3136,256]{1,0:T(8,128)(2,1)} %bitcast.14), channel_id=1, source_target_pairs={{0,8},{1,3},{2,10},{3,5},{4,12},{5,7},{6,14},{7,1},{8,16},{9,11},{... | collective-permute-start | bytes 4816904 | tf_op jit(solution)/shard_map/ppermute | solution.py:35
  12.2 16.4 %collective-permute-start.5 = (bf16[64,512]{1,0:T(8,128)(2,1)}, bf16[64,512]{1,0:T(8,128)(2,1)S(1)}, u32[]{:S(2)}, u32[]{:S(2)}) collective-permute-start(bf16[64,512]{1,0:T(8,128)(2,1)} %get-tuple-element.54.refs_7_.refs_6_), channel_id=1, source_target_pairs={{0,2},{1,9},{2,4},{3,11},{4,6},{5,13},{6,0},{7,15},{8,10},{9,17},{... | collective-permute-start | bytes 196616 | tf_op jit(solution)/shard_map/ppermute | solution.py:39
  13.1 15.6 %collective-permute-start.4 = (bf16[64,512]{1,0:T(8,128)(2,1)}, bf16[64,512]{1,0:T(8,128)(2,1)S(1)}, u32[]{:S(2)}, u32[]{:S(2)}) collective-permute-start(bf16[64,512]{1,0:T(8,128)(2,1)} %get-tuple-element.54.refs_7_.refs_6_), channel_id=1, source_target_pairs={{0,4},{1,17},{2,6},{3,19},{4,0},{5,21},{6,2},{7,23},{8,12},{9,25},... | collective-permute-start | bytes 196616 | tf_op jit(solution)/shard_map/ppermute | solution.py:39
  16.4 12.3 %collective-permute-start.3 = (bf16[64,512]{1,0:T(8,128)(2,1)}, bf16[64,512]{1,0:T(8,128)(2,1)S(1)}, u32[]{:S(2)}, u32[]{:S(2)}) collective-permute-start(bf16[64,512]{1,0:T(8,128)(2,1)} %get-tuple-element.54.refs_7_.refs_6_), channel_id=1, source_target_pairs={{0,6},{1,25},{2,0},{3,27},{4,2},{5,29},{6,4},{7,31},{8,14},{9,1},{... | collective-permute-start | bytes 196616 | tf_op jit(solution)/shard_map/ppermute | solution.py:39
  30.3 11.2 %all-to-all-start.1 = ((f32[16,16,128]{2,1,0:T(8,128)}), f32[16,16,128]{2,1,0:T(8,128)S(1)}, u32[]{:S(2)}, u32[]{:S(2)}) async-start(f32[16,16,128]{2,1,0:T(8,128)} %near_merge.1), calls=%async_computation.1 | async-start | bytes 262144 | tf_op jit(solution)/shard_map/all_to_all | solution.py:442
  35.8 36.9 %collective-permute-start.14 = (bf16[1568,256]{1,0:T(8,128)(2,1)}, bf16[1568,256]{1,0:T(8,128)(2,1)}, u32[]{:S(2)}, u32[]{:S(2)}) collective-permute-start(bf16[1568,256]{1,0:T(8,128)(2,1)} %slice.9), channel_id=1, source_target_pairs={{0,24},{1,7},{2,26},{3,1},{4,28},{5,3},{6,30},{7,5},{8,0},{9,15},{... | collective-permute-start | bytes 2408456 | tf_op jit(solution)/shard_map/ppermute | solution.py:35
  39.4 34.9 %collective-permute-start.13 = (bf16[1568,256]{1,0:T(8,128)(2,1)}, bf16[1568,256]{1,0:T(8,128)(2,1)}, u32[]{:S(2)}, u32[]{:S(2)}) collective-permute-start(bf16[1568,256]{1,0:T(8,128)(2,1)} %slice.8), channel_id=1, source_target_pairs={{0,8},{1,3},{2,10},{3,5},{4,12},{5,7},{6,14},{7,1},{8,16},{9,11},{... | collective-permute-start | bytes 2408456 | tf_op jit(solution)/shard_map/ppermute | solution.py:35
  60.2 10.7 %collective-permute-start.7 = (bf16[3,32,3200]{2,1,0:T(8,128)(2,1)}, bf16[3,32,3200]{2,1,0:T(8,128)(2,1)S(1)}, u32[]{:S(2)}, u32[]{:S(2)}) collective-permute-start(bf16[3,32,3200]{2,1,0:T(8,128)(2,1)} %get-tuple-element.60), channel_id=1, source_target_pairs={{0,2},{1,9},{2,4},{3,11},{4,6},{5,13},{6,0},{7,15},{8,10},{9,17},{... | collective-permute-start | bytes 1843208 | tf_op jit(solution)/shard_map/ppermute | solution.py:39
  60.4 30.5 %collective-permute-start.8 = (bf16[3,32,3200]{2,1,0:T(8,128)(2,1)}, bf16[3,32,3200]{2,1,0:T(8,128)(2,1)S(1)}, u32[]{:S(2)}, u32[]{:S(2)}) collective-permute-start(bf16[3,32,3200]{2,1,0:T(8,128)(2,1)} %get-tuple-element.61), channel_id=1, source_target_pairs={{0,3},{1,8},{2,5},{3,10},{4,7},{5,12},{6,1},{7,14},{8,11},{9,16},{... | collective-permute-start | bytes 1843208 | tf_op jit(solution)/shard_map/ppermute | solution.py:39
  62.1 29.0 %collective-permute-start.9 = (bf16[3,32,3200]{2,1,0:T(8,128)(2,1)}, bf16[3,32,3200]{2,1,0:T(8,128)(2,1)S(1)}, u32[]{:S(2)}, u32[]{:S(2)}) collective-permute-start(bf16[3,32,3200]{2,1,0:T(8,128)(2,1)} %get-tuple-element.62), channel_id=1, source_target_pairs={{0,4},{1,17},{2,6},{3,19},{4,0},{5,21},{6,2},{7,23},{8,12},{9,25},... | collective-permute-start | bytes 1843208 | tf_op jit(solution)/shard_map/ppermute | solution.py:39
  70.9 30.3 %collective-permute-start.10 = (bf16[3,32,3200]{2,1,0:T(8,128)(2,1)}, bf16[3,32,3200]{2,1,0:T(8,128)(2,1)S(1)}, u32[]{:S(2)}, u32[]{:S(2)}) collective-permute-start(bf16[3,32,3200]{2,1,0:T(8,128)(2,1)} %get-tuple-element.63), channel_id=1, source_target_pairs={{0,5},{1,16},{2,7},{3,18},{4,1},{5,20},{6,3},{7,22},{8,13},{9,24},... | collective-permute-start | bytes 1843208 | tf_op jit(solution)/shard_map/ppermute | solution.py:39
  72.7 30.0 %collective-permute-start.11 = (bf16[3,32,3200]{2,1,0:T(8,128)(2,1)}, bf16[3,32,3200]{2,1,0:T(8,128)(2,1)}, u32[]{:S(2)}, u32[]{:S(2)}) collective-permute-start(bf16[3,32,3200]{2,1,0:T(8,128)(2,1)} %get-tuple-element.64), channel_id=1, source_target_pairs={{0,6},{1,25},{2,0},{3,27},{4,2},{5,29},{6,4},{7,31},{8,14},{9,1},{... | collective-permute-start | bytes 1843208 | tf_op jit(solution)/shard_map/ppermute | solution.py:39
  74.3 28.6 %collective-permute-start.12 = (bf16[3,32,3200]{2,1,0:T(8,128)(2,1)}, bf16[3,32,3200]{2,1,0:T(8,128)(2,1)}, u32[]{:S(2)}, u32[]{:S(2)}) collective-permute-start(bf16[3,32,3200]{2,1,0:T(8,128)(2,1)} %get-tuple-element.65), channel_id=1, source_target_pairs={{0,7},{1,24},{2,1},{3,26},{4,3},{5,28},{6,5},{7,30},{8,15},{9,0},{... | collective-permute-start | bytes 1843208 | tf_op jit(solution)/shard_map/ppermute | solution.py:39
  90.9 25.4 %collective-permute-start.15 = (bf16[1,32,3200]{2,1,0:T(8,128)(2,1)}, bf16[1,32,3200]{2,1,0:T(8,128)(2,1)S(1)}, u32[]{:S(2)}, u32[]{:S(2)}) collective-permute-start(bf16[1,32,3200]{2,1,0:T(8,128)(2,1)} %get-tuple-element.68), channel_id=1, source_target_pairs={{0,1},{1,0},{2,3},{3,2},{4,5},{5,4},{6,7},{7,6},{8,9},{9,8},{10,11... | collective-permute-start | bytes 614408 | tf_op jit(solution)/shard_map/ppermute | solution.py:39
  91.1 27.0 %collective-permute-start.16 = (bf16[1,32,3200]{2,1,0:T(8,128)(2,1)}, bf16[1,32,3200]{2,1,0:T(8,128)(2,1)S(1)}, u32[]{:S(2)}, u32[]{:S(2)}) collective-permute-start(bf16[1,32,3200]{2,1,0:T(8,128)(2,1)} %get-tuple-element.69), channel_id=1, source_target_pairs={{0,2},{1,9},{2,4},{3,11},{4,6},{5,13},{6,0},{7,15},{8,10},{9,17},{... | collective-permute-start | bytes 614408 | tf_op jit(solution)/shard_map/ppermute | solution.py:39
  102.9 5.9 %collective-permute-start.24 = (f32[32,128]{1,0:T(8,128)}, f32[32,128]{1,0:T(8,128)S(1)}, u32[]{:S(2)}, u32[]{:S(2)}) collective-permute-start(f32[32,128]{1,0:T(8,128)} %get-tuple-element.79), channel_id=1, source_target_pairs={{0,3},{1,8},{2,5},{3,10},{4,7},{5,12},{6,1},{7,14},{8,11},{9,16},{... | collective-permute-start | bytes 49160 | tf_op jit(solution)/shard_map/ppermute | solution.py:39
  103.8 6.7 %collective-permute-start.25 = (f32[32,128]{1,0:T(8,128)}, f32[32,128]{1,0:T(8,128)S(1)}, u32[]{:S(2)}, u32[]{:S(2)}) collective-permute-start(f32[32,128]{1,0:T(8,128)} %get-tuple-element.80), channel_id=1, source_target_pairs={{0,4},{1,17},{2,6},{3,19},{4,0},{5,21},{6,2},{7,23},{8,12},{9,25},... | collective-permute-start | bytes 49160 | tf_op jit(solution)/shard_map/ppermute | solution.py:39
  110.5 5.7 %collective-permute-start.28 = (f32[32,128]{1,0:T(8,128)}, f32[32,128]{1,0:T(8,128)S(1)}, u32[]{:S(2)}, u32[]{:S(2)}) collective-permute-start(f32[32,128]{1,0:T(8,128)} %get-tuple-element.83), channel_id=1, source_target_pairs={{0,7},{1,24},{2,1},{3,26},{4,3},{5,28},{6,5},{7,30},{8,15},{9,0},{... | collective-permute-start | bytes 49160 | tf_op jit(solution)/shard_map/ppermute | solution.py:39
  112.2 7.4 %collective-permute-start.17 = (bf16[1,32,3200]{2,1,0:T(8,128)(2,1)}, bf16[1,32,3200]{2,1,0:T(8,128)(2,1)S(1)}, u32[]{:S(2)}, u32[]{:S(2)}) collective-permute-start(bf16[1,32,3200]{2,1,0:T(8,128)(2,1)} %get-tuple-element.70), channel_id=1, source_target_pairs={{0,3},{1,8},{2,5},{3,10},{4,7},{5,12},{6,1},{7,14},{8,11},{9,16},{... | collective-permute-start | bytes 614408 | tf_op jit(solution)/shard_map/ppermute | solution.py:39
  113.0 9.1 %collective-permute-start.18 = (bf16[1,32,3200]{2,1,0:T(8,128)(2,1)}, bf16[1,32,3200]{2,1,0:T(8,128)(2,1)S(1)}, u32[]{:S(2)}, u32[]{:S(2)}) collective-permute-start(bf16[1,32,3200]{2,1,0:T(8,128)(2,1)} %get-tuple-element.71), channel_id=1, source_target_pairs={{0,4},{1,17},{2,6},{3,19},{4,0},{5,21},{6,2},{7,23},{8,12},{9,25},... | collective-permute-start | bytes 614408 | tf_op jit(solution)/shard_map/ppermute | solution.py:39
  116.2 8.0 %collective-permute-start.19 = (bf16[1,32,3200]{2,1,0:T(8,128)(2,1)}, bf16[1,32,3200]{2,1,0:T(8,128)(2,1)S(1)}, u32[]{:S(2)}, u32[]{:S(2)}) collective-permute-start(bf16[1,32,3200]{2,1,0:T(8,128)(2,1)} %get-tuple-element.72), channel_id=1, source_target_pairs={{0,5},{1,16},{2,7},{3,18},{4,1},{5,20},{6,3},{7,22},{8,13},{9,24},... | collective-permute-start | bytes 614408 | tf_op jit(solution)/shard_map/ppermute | solution.py:39
  116.3 7.9 %collective-permute-start.20 = (bf16[1,32,3200]{2,1,0:T(8,128)(2,1)}, bf16[1,32,3200]{2,1,0:T(8,128)(2,1)S(1)}, u32[]{:S(2)}, u32[]{:S(2)}) collective-permute-start(bf16[1,32,3200]{2,1,0:T(8,128)(2,1)} %get-tuple-element.73), channel_id=1, source_target_pairs={{0,6},{1,25},{2,0},{3,27},{4,2},{5,29},{6,4},{7,31},{8,14},{9,1},{... | collective-permute-start | bytes 614408 | tf_op jit(solution)/shard_map/ppermute | solution.py:39
  118.1 8.7 %collective-permute-start.21 = (bf16[1,32,3200]{2,1,0:T(8,128)(2,1)}, bf16[1,32,3200]{2,1,0:T(8,128)(2,1)S(1)}, u32[]{:S(2)}, u32[]{:S(2)}) collective-permute-start(bf16[1,32,3200]{2,1,0:T(8,128)(2,1)} %get-tuple-element.74), channel_id=1, source_target_pairs={{0,7},{1,24},{2,1},{3,26},{4,3},{5,28},{6,5},{7,30},{8,15},{9,0},{... | collective-permute-start | bytes 614408 | tf_op jit(solution)/shard_map/ppermute | solution.py:39
  (32 other events, 387.9 us)
where the time goes:
time: 136 us; the launch traced here: 135 us
  starting transfers between devices  40.3 us (30%)
  Pallas kernels  39 us (29%)
  waiting for transfers between devices  30.5 us (22%)
  blocking collectives  20.2 us (15%)
  local copies, waits for them, and re-layouts  3.98 us (3%)
    ppermute x24, starting transfers between devices, exchange_step(): return lax.ppermute(values, PLANE, along(step, 'y', flip))  28.8 us
    ppermute x24, waiting for transfers between devices, exchange_step(): return lax.ppermute(values, PLANE, along(step, 'y', flip))  27.6 us
    pallas_call x2, Pallas kernels, second_values(): pl.pallas_call(make_second_kernel(tuple(cuts), order, pixels, tiles, lane...  20.6 us
    all_to_all x2, blocking collectives, trade(): lax.all_to_all(messages, axes, split_axis=0, concat_axis=0, tiled=True)  20.2 us
    pallas_call x1, Pallas kernels, last_pass(): pl.pallas_call(make_last_kernel(chip_lanes), out_shape=[jax.ShapeDtypeStr...  7.51 us
    ppermute x4, starting transfers between devices, gather_step(): return lax.ppermute(values, PLANE, along(step, 'x', 0))  6.45 us
    pallas_call x1, Pallas kernels, first_sums(): pl.pallas_call(first_kernel, out_shape=[jax.ShapeDtypeStruct((members, 16...  5.59 us
    all_to_all x1, starting transfers between devices, trade(): lax.all_to_all(messages, axes, split_axis=0, concat_axis=0, tiled=True)  4.45 us
  transfers between devices with their start and end apart: 30, of which 10 were waited for; matrix products, arithmetic and copies ran while one was open for 2% of the time, Pallas kernels for 23%

commit v1 on v0

v1 whole, which is shorter than its diff:
```python
import jax
import jax.numpy as jnp
from jax import lax
from jax.experimental import pallas as pl
from jax.experimental.pallas import tpu as pltpu
from jax.sharding import Mesh
from jax.sharding import PartitionSpec as P


EPS = 1e-05
EVERY = ("z", "x", "y", "c")
PLANE = ("x", "y", "c")
RING = 4
MIB = 1 << 20
BAND = 128
HALF = BAND // 2
PIECE = 512


def place(x, y, c):
    return ((x % RING) * RING + y % RING) * 2 + c


def along(step, core0_axis, flip):
    pairs = []
    for x in range(RING):
        for y in range(RING):
            for c in range(2):
                on_x = (core0_axis == "x") == (c == 0)
                there = (x + step, y) if on_x else (x, y + step)
                pairs.append((place(x, y, c), place(*there, c ^ flip)))
    return pairs


def gather_step(values, step):
    return lax.ppermute(values, PLANE, along(step, "x", 0))


def exchange_step(values, step, flip):
    return lax.ppermute(values, PLANE, along(step, "y", flip))


def spot():
    return tuple(lax.axis_index(axis) for axis in PLANE)


def tissue_of(tissue_ref, chip_x, chip_y, core, tiles):
    base = place(chip_x, chip_y, core) * tiles
    return [tissue_ref[base + t].astype(jnp.float32) for t in range(tiles)]


def ring_spot(slot):
    x, y, c = spot()
    along_x, along_y = (1 - c) * slot, c * slot
    return (x + RING - along_x) % RING, (y + RING - along_y) % RING, c


def merge(counts, means, squares):
    total = jnp.sum(counts, axis=0)
    centre = means[0]
    mean_val = centre + jnp.sum(counts * (means - centre), axis=0) / jnp.maximum(total, 1.0)
    spread = jnp.sum(squares + counts * (means - mean_val) ** 2, axis=0)
    return total, mean_val, spread


def local_moments(count, centre, sums, squares):
    safe = jnp.maximum(count, 1.0)
    return centre + sums / safe, squares - sums * sums / safe


def first_kernel(tissue_ref, rows_ref, weight_ref, own_ref, mate_ref, out_ref, turned_ref, pair_ref, acc_ref):
    step = pl.program_id(0)
    tiles = pl.num_programs(0)
    pixels = rows_ref.shape[0]
    width = weight_ref.shape[1]
    base = place(*spot()) * tiles
    held = tissue_ref[base + step].astype(jnp.float32)
    chunk = pixels // 7

    def part(i):
        return jnp.dot(
            rows_ref[i * chunk : (i + 1) * chunk, :],
            weight_ref[...],
            preferred_element_type=jnp.float32,
        )

    @pl.when(step == 0)
    def _():
        acc_ref[...] = jnp.zeros_like(acc_ref)
        acc_ref[0] = jnp.broadcast_to(jnp.mean(part(0), axis=0, keepdims=True), (8, width))
        turned_ref[...] = weight_ref[...].T
        half = own_ref.shape[0]
        pair_ref[:half, :] = own_ref[...]
        pair_ref[half:, :] = mate_ref[...]

    centre = acc_ref[0]
    sums = jnp.zeros((8, width), jnp.float32)
    squares = jnp.zeros((8, width), jnp.float32)
    for i in range(7):
        centred = part(i).reshape(chunk // 8, 8, width) - centre
        sums += jnp.sum(centred, axis=0)
        squares += jnp.sum(centred * centred, axis=0)
    acc_ref[1] += held * sums
    acc_ref[2] += held * squares
    acc_ref[3] += jnp.full((8, width), held * pixels, jnp.float32)

    @pl.when(step == tiles - 1)
    def _():
        count = acc_ref[3, 0:1, :]
        mean, spread = local_moments(
            count,
            acc_ref[0, 0:1, :],
            jnp.sum(acc_ref[1], axis=0, keepdims=True),
            jnp.sum(acc_ref[2], axis=0, keepdims=True),
        )
        parts = width // BAND
        for r, row in enumerate((count, mean, spread)):
            for q in range(parts):
                out_ref[:, r * parts + q, :] = jnp.broadcast_to(
                    row[:, q * BAND : (q + 1) * BAND], (out_ref.shape[0], BAND)
                )


def first_sums(tissue, rows, weight, own, mate, members):
    tiles, pixels, depth = rows.shape
    width = weight.shape[1]
    whole = lambda shape: pl.BlockSpec(shape, lambda i, t: (0,) * len(shape))
    return pl.pallas_call(
        first_kernel,
        out_shape=[
            jax.ShapeDtypeStruct((members, 16, BAND), jnp.float32),
            jax.ShapeDtypeStruct((width, depth), jnp.bfloat16),
            jax.ShapeDtypeStruct((2 * own.shape[0], own.shape[1]), jnp.bfloat16),
        ],
        grid_spec=pltpu.PrefetchScalarGridSpec(
            num_scalar_prefetch=1,
            grid=(tiles,),
            in_specs=[
                pl.BlockSpec((None, pixels, depth), lambda i, t: (i, 0, 0)),
                whole(weight.shape),
                whole(own.shape),
                whole(mate.shape),
            ],
            out_specs=[
                whole((members, 16, BAND)),
                whole((width, depth)),
                whole((2 * own.shape[0], own.shape[1])),
            ],
            scratch_shapes=[pltpu.VMEM((4, 8, width), jnp.float32)],
        ),
        compiler_params=pltpu.CompilerParams(dimension_semantics=("arbitrary",)),
        name="first_sums",
    )(tissue, rows, weight, own, mate)


def near_merge_kernel(in_ref, out_ref):
    parts = 4
    got = in_ref[...]
    rows = merge(*(got[:, r * parts : (r + 1) * parts, :] for r in range(3)))
    for r, row in enumerate(rows):
        out_ref[:, r * parts : (r + 1) * parts, :] = jnp.broadcast_to(
            row[None], (out_ref.shape[0], parts, BAND)
        )


def near_merge(messages, members):
    return pl.pallas_call(
        near_merge_kernel,
        out_shape=jax.ShapeDtypeStruct((members, 16, BAND), jnp.float32),
        compiler_params=pltpu.CompilerParams(vmem_limit_bytes=4 * MIB),
        name="near_merge",
    )(messages)


def first_norm(in_ref, gain_ref, bias_ref, scale_col, shift_col):
    parts = gain_ref.shape[0]
    got = in_ref[...]
    count, mean, spread = merge(*(got[:, r * parts : (r + 1) * parts, :] for r in range(3)))
    var = spread / count
    scale = gain_ref[...] * lax.rsqrt(var + EPS)
    for value, col in ((scale, scale_col), (bias_ref[...] - mean * scale, shift_col)):
        for q in range(parts):
            col[q * BAND : (q + 1) * BAND, :] = jnp.broadcast_to(value[q : q + 1, :], (BAND, BAND)).T
    return mean, var


def make_second_kernel(order, pixels, tiles, lanes, last):
    n_in = slots = len(order)
    early = 2 * PIECE

    def kernel(tissue_ref, *refs):
        inputs = refs[:n_in]
        w1_ref, moments_ref, gain_ref, bias_ref = refs[n_in : n_in + 4]
        w2_refs = refs[n_in + 4 : n_in + 8]
        rest = refs[n_in + 8 :]
        if last:
            before_ref, rest = rest[0], rest[1:]
        outs, stats_ref, rest = rest[:8], rest[8], rest[9:]
        if not last:
            mean_ref, var_ref, rest = rest[0], rest[1], rest[2:]
        rows, w2_ref, scale_ref, shift_ref, buffer, sems, out_sems = rest
        core = lax.axis_index("c")
        shift = pl.multiple_of(core * HALF, HALF)

        def load(slot, part):
            start = part * early
            size = lanes - HALF - early if part else early
            return pltpu.make_async_copy(
                inputs[slot].at[pl.ds(start, size), :],
                rows.at[slot, pl.ds(pl.multiple_of(shift + start, 16), size), :],
                sems.at[slot, part],
            )

        for slot in range(slots):
            for part in range(2):
                load(slot, part).start()
            rest_at = pl.multiple_of((1 - core) * (lanes - HALF), HALF)
            rows[slot, pl.ds(rest_at, HALF), :] = jnp.zeros((HALF, rows.shape[2]), rows.dtype)
        for i, ref in enumerate(w2_refs):
            w2_ref[i * ref.shape[0] : (i + 1) * ref.shape[0], :] = ref[...]
        mean, var = first_norm(moments_ref, gain_ref, bias_ref, scale_ref, shift_ref)
        if not last:
            mean_ref[...] = mean
            var_ref[...] = var
        width = outs[0].shape[1]

        def out_copies(slot, part):
            at = part * lanes // 2 // PIECE * PIECE
            size = lanes - at if part else lanes // 2 // PIECE * PIECE
            return [
                pltpu.make_async_copy(
                    buffer.at[i, slot, :, pl.ds(at, size)],
                    outs[i].at[slot, :, pl.ds(at, size)],
                    out_sems.at[i, slot, part],
                )
                for i in range(8)
            ]

        centre = jnp.broadcast_to(before_ref[:, 0:1], (8 * width, BAND)) if last else None
        sums = squares = None
        for slot in range(slots):
            held_here = tissue_of(tissue_ref, *ring_spot(order[slot]), tiles)
            load(slot, 0).wait()
            for at in range(0, lanes, PIECE):
                if at == early:
                    load(slot, 1).wait()
                tile = min(PIECE, lanes - at)
                wide = lambda v: jnp.concatenate([v] * (tile // BAND), axis=1)
                block = rows[slot, at : at + tile, :]
                first = lax.dot_general(
                    w1_ref[...],
                    block,
                    (((1,), (1,)), ((), ())),
                    preferred_element_type=jnp.float32,
                )
                activation = jnp.maximum(
                    (first * wide(scale_ref[...]) + wide(shift_ref[...])).astype(jnp.bfloat16), 0
                )
                second = jnp.dot(w2_ref[...], activation, preferred_element_type=jnp.float32)
                if centre is None:
                    centre = jnp.broadcast_to(
                        jnp.mean(second[:, BAND:], axis=1, keepdims=True), (8 * width, BAND)
                    )
                second = second - wide(centre)
                lane = lax.broadcasted_iota(jnp.int32, (1, tile), 1) + (at - shift)
                held = jnp.zeros((1, tile), jnp.float32)
                for t in range(tiles):
                    inside = (lane >= t * pixels) & (lane < (t + 1) * pixels)
                    held += jnp.where(inside, held_here[t], 0.0)
                kept = second * held
                squared = kept * second
                part = sum(kept[:, i * BAND : (i + 1) * BAND] for i in range(tile // BAND))
                part2 = sum(squared[:, i * BAND : (i + 1) * BAND] for i in range(tile // BAND))
                sums = part if sums is None else sums + part
                squares = part2 if squares is None else squares + part2
                rounded = second.astype(jnp.bfloat16)
                for i in range(8):
                    buffer[i, slot, :, at : at + tile] = rounded[i * width : (i + 1) * width, :]
                if at + tile == lanes // 2 // PIECE * PIECE:
                    for copy in out_copies(slot, 0):
                        copy.start()
            for copy in out_copies(slot, 1):
                copy.start()
        lane = lax.broadcasted_iota(jnp.int32, (8 * width, BAND), 1)
        sums = jnp.sum(sums, axis=1, keepdims=True)
        squares = jnp.sum(squares, axis=1, keepdims=True)
        if last:
            count = sum(
                held for slot in range(RING) for held in tissue_of(tissue_ref, *ring_spot(slot), tiles)
            )
            count = jnp.full((8 * width, 1), count * pixels, jnp.float32)
            mean, spread = local_moments(
                count, before_ref[:, 0:1], before_ref[:, 1:2] + sums, before_ref[:, 2:3] + squares
            )
            message = jnp.where(lane == 0, count, jnp.where(lane == 1, mean, spread)).T[:8, :]
            stats_ref[...] = message
        else:
            stats_ref[...] = jnp.where(lane == 0, centre, jnp.where(lane == 1, sums, squares))
        for slot in range(slots):
            for part in range(2):
                for copy in out_copies(slot, part):
                    copy.wait()

    return kernel


def second_values(tissue, inputs, order, norm, pairs, before, pixels, tiles):
    depth = norm[0].shape[1]
    lanes = pixels * tiles + HALF
    channels = sum(pair.shape[0] for pair in pairs)
    vmem = pl.BlockSpec(memory_space=pltpu.VMEM)
    anywhere = pl.BlockSpec(memory_space=pl.ANY)
    extra = [] if before is None else [before]
    hidden = norm[0].shape[0]
    row = jax.ShapeDtypeStruct((hidden // BAND, BAND), jnp.float32)
    rows_out = [row, row] if before is None else []
    stats = (channels, BAND) if before is None else (8, channels)
    outs = pl.pallas_call(
        make_second_kernel(order, pixels, tiles, lanes, before is not None),
        out_shape=[jax.ShapeDtypeStruct((len(inputs), channels // 8, lanes), jnp.bfloat16)] * 8
        + [jax.ShapeDtypeStruct(stats, jnp.float32), *rows_out],
        in_specs=[pl.BlockSpec(memory_space=pltpu.SMEM)]
        + [pl.BlockSpec(memory_space=pl.ANY)] * len(inputs)
        + [vmem] * (8 + len(extra)),
        out_specs=[anywhere] * 8 + [vmem] * (1 + len(rows_out)),
        scratch_shapes=[
            pltpu.VMEM((len(inputs), lanes, depth), jnp.bfloat16),
            pltpu.VMEM((channels, hidden), jnp.bfloat16),
            pltpu.VMEM((hidden, BAND), jnp.float32),
            pltpu.VMEM((hidden, BAND), jnp.float32),
            pltpu.VMEM((8, len(inputs), channels // 8, lanes), jnp.bfloat16),
            pltpu.SemaphoreType.DMA((len(inputs), 2)),
            pltpu.SemaphoreType.DMA((8, len(inputs), 2)),
        ],
        compiler_params=pltpu.CompilerParams(
            vmem_limit_bytes=(16 + 6 * len(inputs)) * MIB
        ),
        name="second_values",
    )(tissue, *inputs, *norm, *pairs, *extra)
    return outs[:8], *outs[8:]


def stamp_kernel(*refs):
    messages, before_ref, refs = refs[:RING], refs[RING], refs[RING + 1 :]
    blocks, all_ref, buffer, in_sems, out_sems = refs[8:16], refs[16], refs[17], refs[18], refs[19]
    z = lax.axis_index("z")
    for step, ref in enumerate(messages):
        all_ref[(z + RING - step) % RING] = ref[...]
    core = lax.axis_index("c")
    lanes = blocks[0].shape[2]
    spare = pl.ds(pl.multiple_of((1 - core) * (lanes - BAND), BAND), BAND)
    loads = [
        pltpu.make_async_copy(block.at[0, :, spare], buffer.at[i], in_sems.at[i])
        for i, block in enumerate(blocks)
    ]
    stores = [
        pltpu.make_async_copy(buffer.at[i], block.at[0, :, spare], out_sems.at[i])
        for i, block in enumerate(blocks)
    ]
    for copy in loads:
        copy.start()
    got = all_ref[...]
    channels = got.shape[2]
    rows = merge(got[:, 0:1, :], got[:, 1:2, :], got[:, 2:3, :])
    turned = jnp.concatenate([*rows, jnp.zeros((BAND - 3, channels), jnp.float32)], axis=0).T
    lane = lax.broadcasted_iota(jnp.int32, turned.shape, 1) - (1 - core) * HALF
    value = jnp.broadcast_to(before_ref[:, 0:1], turned.shape)
    for q in range(3):
        value = jnp.where(lane % 4 == q, turned[:, q : q + 1], value)
    high = value.astype(jnp.bfloat16).astype(jnp.float32)
    middle = (value - high).astype(jnp.bfloat16).astype(jnp.float32)
    low = value - high - middle
    value = jnp.where(lane < 4, high, jnp.where(lane < 8, middle, low))
    written = (lane >= 0) & (lane < 12)
    width = channels // 8
    for i in range(8):
        loads[i].wait()
        here = slice(i * width, (i + 1) * width)
        buffer[i] = jnp.where(
            written[here], value[here], buffer[i].astype(jnp.float32)
        ).astype(jnp.bfloat16)
        stores[i].start()
    for copy in stores:
        copy.wait()


def stamp(messages, before, blocks):
    vmem = pl.BlockSpec(memory_space=pltpu.VMEM)
    anywhere = pl.BlockSpec(memory_space=pl.ANY)
    width = blocks[0].shape[1]
    return pl.pallas_call(
        stamp_kernel,
        out_shape=[jax.ShapeDtypeStruct(block.shape, block.dtype) for block in blocks],
        in_specs=[vmem] * (RING + 1) + [anywhere] * 8,
        out_specs=[anywhere] * 8,
        scratch_shapes=[
            pltpu.VMEM((RING, *messages[0].shape), jnp.float32),
            pltpu.VMEM((8, width, BAND), jnp.bfloat16),
            pltpu.SemaphoreType.DMA((8,)),
            pltpu.SemaphoreType.DMA((8,)),
        ],
        input_output_aliases={RING + 1 + i: i for i in range(8)},
        compiler_params=pltpu.CompilerParams(vmem_limit_bytes=4 * MIB),
        name="stamp",
    )(*messages, before, *blocks)


def make_last_kernel(lanes, chip_lanes):
    cut = chip_lanes // 2 // BAND * BAND

    def kernel(*refs):
        moved = refs[:16]
        gain_ref, bias_ref, out_ref, mean_ref, var_ref = refs[16:21]
        outbuf, shift_ref, out_sems = refs[21:]
        x, y, core = spot()

        def piece(ring, slot, flip):
            group, row = ((0, 0), (0, 1), (1, 0), (0, 2))[slot]
            return moved[group * 8 + ring * 2 + flip].at[row]

        def store(a, b):
            n = a * RING + b
            chip = ((x + RING - a) % RING) * RING + (y + RING - b) % RING
            return pltpu.make_async_copy(
                outbuf.at[n],
                out_ref.at[:, pl.ds(pl.multiple_of(chip * chip_lanes, BAND), chip_lanes)],
                out_sems.at[n],
            )

        steps = [(a, b) for a in range(RING) for b in range(RING)]
        LAST = 2
        width = moved[0].shape[1]
        lane = lax.broadcasted_iota(jnp.int32, (width, BAND), 1)
        row = lax.broadcasted_iota(jnp.int32, (width, BAND), 0)
        device = place(x, y, core)
        per_row = BAND // width

        def own_channels(ref):
            line = ref[pl.ds(device // per_row, 1), :]
            here = lane == row + (device % per_row) * width
            return jnp.sum(jnp.where(here, line, 0.0), axis=1, keepdims=True)

        gain, bias = own_channels(gain_ref), own_channels(bias_ref)

        def chosen(flip0, flip1):
            return jnp.where(core == 0, flip0.astype(jnp.float32), flip1.astype(jnp.float32))

        ends = (slice(lanes - BAND, lanes), slice(0, BAND))
        notes = []
        for i in range(2):
            for k in range(RING):
                both = [piece(k, LAST, i), piece(k, LAST, 1 - i)]
                notes.append(chosen(*(ref[:, ends[i]] for ref in both)))

        def read(q):
            out = []
            for n, note in enumerate(notes):
                at = q + (HALF if n < RING else 0)
                out.append(note[:, at : at + 1] + note[:, at + 4 : at + 5] + note[:, at + 8 : at + 9])
            return jnp.stack(out)

        count, mean, spread = merge(read(0), read(1), read(2))
        var = spread / count
        centre = read(3)
        slope = gain * lax.rsqrt(var + EPS)
        for n in range(2 * RING):
            shift_ref[n] = jnp.broadcast_to((centre[n] - mean) * slope + bias, (width, BAND))
        scale = jnp.broadcast_to(slope, (width, BAND))
        for value, ref in ((mean, mean_ref), (var, var_ref)):
            line = jnp.sum(jnp.where(lane == row, value, 0.0), axis=0, keepdims=True)
            ref[...] = line[:, :width]

        def finish(values, shift):
            wide = lambda v: jnp.concatenate([v] * (values.shape[1] // BAND), axis=1)
            return values.astype(jnp.float32) * wide(scale) + wide(shift)

        for c in range(2):

            @pl.when(core == c)
            def _():
                for a, b in steps:
                    n = a * RING + b
                    left_shift = shift_ref[b]
                    right_shift = shift_ref[RING + a]
                    left = piece(b, a, c)
                    right = piece(a, b, 1 - c)
                    middle = jnp.where(
                        lane < HALF,
                        finish(left[:, cut : cut + BAND], left_shift),
                        finish(right[:, :BAND], right_shift),
                    )
                    for at, value in (
                        (0, finish(left[:, :cut], left_shift)),
                        (cut, middle),
                        (cut + BAND, finish(right[:, BAND:], right_shift)),
                    ):
                        outbuf[n, :, at : at + value.shape[1]] = jnp.maximum(
                            value.astype(jnp.bfloat16), 0
                        )
                    store(a, b).start()

        for a, b in steps:
            store(a, b).wait()

    return kernel


def last_pass(moved, gain, bias, chip_lanes):
    _, width, lanes = moved[0].shape
    vmem = pl.BlockSpec(memory_space=pltpu.VMEM)
    hbm = pl.BlockSpec(memory_space=pl.ANY)
    chips = RING * RING
    stat = jax.ShapeDtypeStruct((1, width), jnp.float32)
    return pl.pallas_call(
        make_last_kernel(lanes, chip_lanes),
        out_shape=[jax.ShapeDtypeStruct((width, chips * chip_lanes), jnp.bfloat16), stat, stat],
        in_specs=[vmem] * 18,
        out_specs=[hbm, vmem, vmem],
        scratch_shapes=[
            pltpu.VMEM((chips, width, chip_lanes), jnp.bfloat16),
            pltpu.VMEM((8, width, BAND), jnp.float32),
            pltpu.SemaphoreType.DMA((chips,)),
        ],
        compiler_params=pltpu.CompilerParams(vmem_limit_bytes=24 * MIB),
        name="last_pass",
    )(*moved, gain.reshape(-1, BAND), bias.reshape(-1, BAND))


def trade(messages, axes):
    return lax.all_to_all(messages, axes, split_axis=0, concat_axis=0, tiled=True)


ROUTES = [(step, flip) for step in range(RING) for flip in range(2)]


def send(blocks):
    out = []
    for route, block in zip(ROUTES, blocks):
        if route != (0, 0):
            block = exchange_step(block, *route)
        out.append(block)
    return out


def shards(
    features, tissue, first_weight, first_gain, first_bias, second_weight, second_gain, second_bias
):
    tiles, pixels, depth = features.shape[1:]
    rows = features.reshape(tiles * pixels, depth)
    row_tissue = tissue[0]
    own = second_weight.T
    mate = lax.ppermute(own, "c", [(0, 1), (1, 0)])
    ahead = gather_step(rows, 1)
    behind = gather_step(rows, 3)
    messages, w1t, pair = first_sums(
        row_tissue, features[0], first_weight, own, mate, 2 * RING
    )
    messages = trade(messages, ("z", "c"))
    after, before = exchange_step(pair, 3, 0), exchange_step(pair, 1, 0)
    messages = near_merge(messages, RING * RING)
    messages = trade(messages, ("x", "y"))
    across = exchange_step(pair, 2, 0)
    far = gather_step(rows, 2)
    pairs = [pair, after, across, before]
    norm = [w1t, messages] + [v.reshape(-1, BAND) for v in (first_gain, first_bias)]
    near, sums, first_mean, first_var = second_values(
        row_tissue, [rows, ahead, behind], (0, 1, 3), norm, pairs, None, pixels, tiles
    )
    moved = send(near)
    rest, messages = second_values(row_tissue, [far], (2,), norm, pairs, sums, pixels, tiles)
    messages = [messages] + [
        lax.ppermute(messages, "z", [(i, (i + step) % RING) for i in range(RING)])
        for step in range(1, RING)
    ]
    rest = stamp(messages, sums, rest)
    moved += send(rest)
    output, second_mean, second_var = last_pass(moved, second_gain, second_bias, 2 * tiles * pixels)
    return (
        output[None],
        first_mean.reshape(-1),
        first_var.reshape(-1),
        second_mean[0],
        second_var[0],
    )


def solution(mesh):
    fine = Mesh(mesh.devices.reshape(RING, RING, RING, 2), EVERY)
    in_specs = (
        P("z", PLANE, None, None),
        P("z", None),
        P(),
        P(),
        P(),
        P(None, PLANE),
        P(),
        P(),
    )
    out_specs = (P("z", PLANE, None), P(), P(), P(PLANE), P(PLANE))
    return jax.shard_map(
        shards, mesh=fine, in_specs=in_specs, out_specs=out_specs, check_vma=False
    )
```

time: 136 us -> 141 us (1.037)
  waiting for transfers between devices: 30.5 us -> 65.8 us
  blocking collectives: 20.2 us -> 0 us
  Pallas kernels: 39 us -> 29.5 us
  starting transfers between devices: 40.3 us -> 41.9 us
  local copies, waits for them, and re-layouts: 3.98 us -> 2.41 us
    ppermute x24 -> x17, waiting for transfers between devices: 27.6 us -> 52.3 us  [exchange_step(): return lax.ppermute(values, PLANE, along(step, 'y', flip))]
    all_to_all x2 -> x0, blocking collectives: 20.2 us -> none  [trade(): lax.all_to_all(messages, axes, split_axis=0, concat_axis=0, tiled=True)]
    ppermute x24 -> x17, starting transfers between devices: 28.8 us -> 19.6 us  [exchange_step(): return lax.ppermute(values, PLANE, along(step, 'y', flip))]
    pallas_call x5 -> x4, Pallas kernels: 31.8 us -> 23.6 us  [the longest x2 18.9 us: second_values(): pl.pallas_call(make_second_kernel(order, pixels, tiles, lanes, before is...]
    all_to_all x1 -> x2, waiting for transfers between devices: 1.8 us -> 9.15 us  [trade(): lax.all_to_all(messages, axes, split_axis=0, concat_axis=0, tiled=True)]
    all_to_all x1 -> x2, starting transfers between devices: 4.45 us -> 11.2 us  [trade(): lax.all_to_all(messages, axes, split_axis=0, concat_axis=0, tiled=True)]
    ppermute x0 -> x3, starting transfers between devices: none -> 4.53 us  [shards(): lax.ppermute(messages, 'z', [(i, (i + step) % RING) for i in range(RING)])]
    ppermute x0 -> x3, waiting for transfers between devices: none -> 3.3 us  [shards(): lax.ppermute(messages, 'z', [(i, (i + step) % RING) for i in range(RING)])]
  transfers between devices with their start and end apart: 30 -> 26, of which waited for: 10 -> 14; matrix products, arithmetic and copies ran while one was open for 2% -> 0% of each run, Pallas kernels for 23% -> 14%
where the time goes in v1:
time: 141 us
  waiting for transfers between devices  65.8 us (47%)
  starting transfers between devices  41.9 us (30%)
  Pallas kernels  29.5 us (21%)
  local copies, waits for them, and re-layouts  2.41 us (2%)
    ppermute x17, waiting for transfers between devices, exchange_step(): return lax.ppermute(values, PLANE, along(step, 'y', flip))  52.3 us
    ppermute x17, starting transfers between devices, exchange_step(): return lax.ppermute(values, PLANE, along(step, 'y', flip))  19.6 us
    pallas_call x2, Pallas kernels, second_values(): pl.pallas_call(make_second_kernel(order, pixels, tiles, lanes, before is...  18.9 us
    all_to_all x2, starting transfers between devices, trade(): lax.all_to_all(messages, axes, split_axis=0, concat_axis=0, tiled=True)  11.2 us
    all_to_all x2, waiting for transfers between devices, trade(): lax.all_to_all(messages, axes, split_axis=0, concat_axis=0, tiled=True)  9.15 us
    ppermute x3, starting transfers between devices, gather_step(): return lax.ppermute(values, PLANE, along(step, 'x', 0))  5.27 us
    pallas_call x1, Pallas kernels, first_sums(): pl.pallas_call(first_kernel, out_shape=[jax.ShapeDtypeStruct((members, 16...  5.16 us
    ppermute x3, starting transfers between devices, shards(): lax.ppermute(messages, 'z', [(i, (i + step) % RING) for i in range(RING)])  4.53 us
  transfers between devices with their start and end apart: 26, of which 14 were waited for; matrix products, arithmetic and copies ran while one was open for 0% of the time, Pallas kernels for 14%

profile of v1, /device:TPU:1, one launch (start us, length us, event | category | flops | bytes accessed | tf_op | source)
XLA Modules:
  0.0 140.6 jit_solution(13042162326538009840)
XLA Ops:
  0.7 3.6 %collective-permute-start.1 = (bf16[3136,256]{1,0:T(8,128)(2,1)}, bf16[3136,256]{1,0:T(8,128)(2,1)}, u32[]{:S(2)}, u32[]{:S(2)}) collective-permute-start(bf16[3136,256]{1,0:T(8,128)(2,1)} %bitcast.13), channel_id=1, source_target_pairs={{0,24},{1,7},{2,26},{3,1},{4,28},{5,3},{6,30},{7,5},{8,0},{9,15},{... | collective-permute-start | bytes 4816904 | tf_op jit(solution)/shard_map/ppermute | solution.py:36
  4.3 1.6 %collective-permute-start.13 = (bf16[3136,256]{1,0:T(8,128)(2,1)}, bf16[3136,256]{1,0:T(8,128)(2,1)S(1)}, u32[]{:S(2)}, u32[]{:S(2)}) collective-permute-start(bf16[3136,256]{1,0:T(8,128)(2,1)} %bitcast.15), channel_id=1, source_target_pairs={{0,16},{1,5},{2,18},{3,7},{4,20},{5,1},{6,22},{7,3},{8,24},{9,13},... | collective-permute-start | bytes 4816904 | tf_op jit(solution)/shard_map/ppermute | solution.py:36
  9.0 5.2 %first_sums.1 = (f32[8,16,128]{2,1,0:T(8,128)}, bf16[512,256]{1,0:T(8,128)(2,1)}, bf16[64,512]{1,0:T(8,128)(2,1)}) custom-call(s32[128]{0:T(128)} %bitcast.22, bf16[4,784,256]{2,1,0:T(8,128)(2,1)} %bitcast.16, bf16[256,512]{1,0:T(8,128)(2,1)} %weight_ref.1, bf16[32,512]{1,0:T(8,128)(2,1)} %bitcast.28, bf16[32,512]{1,0:T(8,128)(2,1)} %copy-done.8), custom_call_target="tpu_custom_call" | custom-call | tf_op jit(solution)/shard_map/first_sums/pallas_call | solution.py:128
  14.1 5.7 %all-to-all-start = ((f32[8,16,128]{2,1,0:T(8,128)}), f32[8,16,128]{2,1,0:T(8,128)S(1)}, u32[]{:S(2)}, u32[]{:S(2)}) async-start(f32[8,16,128]{2,1,0:T(8,128)} %get-tuple-element.40), calls=%async_computation | async-start | bytes 131072 | tf_op jit(solution)/shard_map/all_to_all | solution.py:530
  21.3 3.3 %all-to-all-done.in_ref = f32[8,16,128]{2,1,0:T(8,128)S(1)} async-done(((f32[8,16,128]{2,1,0:T(8,128)}), f32[8,16,128]{2,1,0:T(8,128)S(1)}, u32[]{:S(2)}, u32[]{:S(2)}) %all-to-all-start) | async-done | bytes 65568 | tf_op jit(solution)/shard_map/all_to_all | solution.py:530
  25.3 5.5 %all-to-all-start.1 = ((f32[16,16,128]{2,1,0:T(8,128)}), f32[16,16,128]{2,1,0:T(8,128)S(1)}, u32[]{:S(2)}, u32[]{:S(2)}) async-start(f32[16,16,128]{2,1,0:T(8,128)} %near_merge.1), calls=%async_computation.1 | async-start | bytes 262144 | tf_op jit(solution)/shard_map/all_to_all | solution.py:530
  30.9 2.9 %collective-permute-start.4 = (bf16[64,512]{1,0:T(8,128)(2,1)}, bf16[64,512]{1,0:T(8,128)(2,1)S(1)}, u32[]{:S(2)}, u32[]{:S(2)}) collective-permute-start(bf16[64,512]{1,0:T(8,128)(2,1)} %get-tuple-element.41.refs_7_.refs_5_), channel_id=1, source_target_pairs={{0,4},{1,17},{2,6},{3,19},{4,0},{5,21},{6,2},{7,23},{8,12},{9,25},... | collective-permute-start | bytes 196616 | tf_op jit(solution)/shard_map/ppermute | solution.py:40
  34.6 3.4 %collective-permute-done.4.refs_9_.refs_7_ = bf16[64,512]{1,0:T(8,128)(2,1)S(1)} collective-permute-done((bf16[64,512]{1,0:T(8,128)(2,1)}, bf16[64,512]{1,0:T(8,128)(2,1)S(1)}, u32[]{:S(2)}, u32[]{:S(2)}) %collective-permute-start.4) | collective-permute-done | bytes 65568 | tf_op jit(solution)/shard_map/ppermute | solution.py:40
  38.0 4.5 %collective-permute-done.3.refs_8_.refs_6_ = bf16[64,512]{1,0:T(8,128)(2,1)S(1)} collective-permute-done((bf16[64,512]{1,0:T(8,128)(2,1)}, bf16[64,512]{1,0:T(8,128)(2,1)S(1)}, u32[]{:S(2)}, u32[]{:S(2)}) %collective-permute-start.3) | collective-permute-done | bytes 65568 | tf_op jit(solution)/shard_map/ppermute | solution.py:40
  42.5 5.8 %all-to-all-done.1.refs_4_.refs_2_ = f32[16,16,128]{2,1,0:T(8,128)S(1)} async-done(((f32[16,16,128]{2,1,0:T(8,128)}), f32[16,16,128]{2,1,0:T(8,128)S(1)}, u32[]{:S(2)}, u32[]{:S(2)}) %all-to-all-start.1) | async-done | bytes 131104 | tf_op jit(solution)/shard_map/all_to_all | solution.py:530
  50.1 13.6 %second_values.2 = (bf16[3,32,3200]{2,1,0:T(8,128)(2,1)S(1)}, bf16[3,32,3200]{2,1,0:T(8,128)(2,1)S(1)}, bf16[3,32,3200]{2,1,0:T(8,128)(2,1)S(1)}, bf16[3,32,3200...) custom-call(s32[128]{0:T(128)S(1)} %bitcast.23, ...), custom_call_target="tpu_custom_call" | custom-call | tf_op jit(solution)/shard_map/second_values/pallas_call | solution.py:318
  63.8 5.3 %second_values.3 = (bf16[1,32,3200]{2,1,0:T(8,128)(2,1)S(1)}, bf16[1,32,3200]{2,1,0:T(8,128)(2,1)S(1)}, bf16[1,32,3200]{2,1,0:T(8,128)(2,1)S(1)}, bf16[1,32,3200...) custom-call(s32[128]{0:T(128)S(1)} %bitcast.24, ...), custom_call_target="tpu_custom_call" | custom-call | tf_op jit(solution)/shard_map/second_values/pallas_call | solution.py:318
  69.1 3.8 %collective-permute-start.16 = (f32[8,256]{1,0:T(8,128)S(1)}, f32[8,256]{1,0:T(8,128)S(1)}, u32[]{:S(2)}, u32[]{:S(2)}) collective-permute-start(f32[8,256]{1,0:T(8,128)S(1)} %get-tuple-element.51.refs_0_), channel_id=1, source_target_pairs={{0,96},{32,0},{64,32},{96,64},{1,97},{33,1},{65,33},{97,65},{2,98}... | collective-permute-start | bytes 24584 | tf_op jit(solution)/shard_map/ppermute | solution.py:572
  73.7 3.2 %collective-permute-done.15.refs_2_ = f32[8,256]{1,0:T(8,128)S(1)} collective-permute-done((f32[8,256]{1,0:T(8,128)S(1)}, f32[8,256]{1,0:T(8,128)S(1)}, u32[]{:S(2)}, u32[]{:S(2)}) %collective-permute-start.15) | collective-permute-done | bytes 8224 | tf_op jit(solution)/shard_map/ppermute | solution.py:572
  77.5 3.0 %collective-permute-start.17 = (bf16[1,32,3200]{2,1,0:T(8,128)(2,1)S(1)}, bf16[1,32,3200]{2,1,0:T(8,128)(2,1)S(1)}, u32[]{:S(2)}, u32[]{:S(2)}) collective-permute-start(bf16[1,32,3200]{2,1,0:T(8,128)(2,1)S(1)} %get-tuple-element.61), channel_id=1, source_target_pairs={{0,1},{1,0},{2,3},{3,2},{4,5},{5,4},{6,7},{7,6},{8,9},{9,8},{10,11... | collective-permute-start | bytes 614408 | tf_op jit(solution)/shard_map/ppermute | solution.py:40
  81.8 2.8 %collective-permute-start.20 = (bf16[1,32,3200]{2,1,0:T(8,128)(2,1)S(1)}, bf16[1,32,3200]{2,1,0:T(8,128)(2,1)S(1)}, u32[]{:S(2)}, u32[]{:S(2)}) collective-permute-start(bf16[1,32,3200]{2,1,0:T(8,128)(2,1)S(1)} %get-tuple-element.64), channel_id=1, source_target_pairs={{0,4},{1,17},{2,6},{3,19},{4,0},{5,21},{6,2},{7,23},{8,12},{9,25},... | collective-permute-start | bytes 614408 | tf_op jit(solution)/shard_map/ppermute | solution.py:40
  84.5 8.8 %collective-permute-done.18.refs_10_ = bf16[1,32,3200]{2,1,0:T(8,128)(2,1)S(1)} collective-permute-done((bf16[1,32,3200]{2,1,0:T(8,128)(2,1)S(1)}, bf16[1,32,3200]{2,1,0:T(8,128)(2,1)S(1)}, u32[]{:S(2)}, u32[]{:S(2)}) %collective-permute-start.18) | collective-permute-done | bytes 204832 | tf_op jit(solution)/shard_map/ppermute | solution.py:40
  94.6 6.2 %collective-permute-done.19.refs_11_ = bf16[1,32,3200]{2,1,0:T(8,128)(2,1)S(1)} collective-permute-done((bf16[1,32,3200]{2,1,0:T(8,128)(2,1)S(1)}, bf16[1,32,3200]{2,1,0:T(8,128)(2,1)S(1)}, u32[]{:S(2)}, u32[]{:S(2)}) %collective-permute-start.19) | collective-permute-done | bytes 204832 | tf_op jit(solution)/shard_map/ppermute | solution.py:40
  102.0 3.7 %collective-permute-done.22.refs_14_ = bf16[1,32,3200]{2,1,0:T(8,128)(2,1)S(1)} collective-permute-done((bf16[1,32,3200]{2,1,0:T(8,128)(2,1)S(1)}, bf16[1,32,3200]{2,1,0:T(8,128)(2,1)S(1)}, u32[]{:S(2)}, u32[]{:S(2)}) %collective-permute-start.22) | collective-permute-done | bytes 204832 | tf_op jit(solution)/shard_map/ppermute | solution.py:40
  108.1 3.1 %collective-permute-start.11 = (bf16[3,32,3200]{2,1,0:T(8,128)(2,1)S(1)}, bf16[3,32,3200]{2,1,0:T(8,128)(2,1)S(1)}, u32[]{:S(2)}, u32[]{:S(2)}) collective-permute-start(bf16[3,32,3200]{2,1,0:T(8,128)(2,1)S(1)} %get-tuple-element.48), channel_id=1, source_target_pairs={{0,6},{1,25},{2,0},{3,27},{4,2},{5,29},{6,4},{7,31},{8,14},{9,1},{... | collective-permute-start | bytes 1843208 | tf_op jit(solution)/shard_map/ppermute | solution.py:40
  111.3 13.6 %collective-permute-done.8.refs_3_ = bf16[3,32,3200]{2,1,0:T(8,128)(2,1)S(1)} collective-permute-done((bf16[3,32,3200]{2,1,0:T(8,128)(2,1)S(1)}, bf16[3,32,3200]{2,1,0:T(8,128)(2,1)S(1)}, u32[]{:S(2)}, u32[]{:S(2)}) %collective-permute-start.8) | collective-permute-done | bytes 614432 | tf_op jit(solution)/shard_map/ppermute | solution.py:40
  124.9 3.4 %collective-permute-done.11.refs_6_ = bf16[3,32,3200]{2,1,0:T(8,128)(2,1)S(1)} collective-permute-done((bf16[3,32,3200]{2,1,0:T(8,128)(2,1)S(1)}, bf16[3,32,3200]{2,1,0:T(8,128)(2,1)S(1)}, u32[]{:S(2)}, u32[]{:S(2)}) %collective-permute-start.11) | collective-permute-done | bytes 614432 | tf_op jit(solution)/shard_map/ppermute | solution.py:40
  128.3 8.0 %collective-permute-done.12.refs_7_ = bf16[3,32,3200]{2,1,0:T(8,128)(2,1)S(1)} collective-permute-done((bf16[3,32,3200]{2,1,0:T(8,128)(2,1)S(1)}, bf16[3,32,3200]{2,1,0:T(8,128)(2,1)S(1)}, u32[]{:S(2)}, u32[]{:S(2)}) %collective-permute-start.12) | collective-permute-done | bytes 614432 | tf_op jit(solution)/shard_map/ppermute | solution.py:40
  136.3 4.1 %last_pass.1 = (bf16[32,100352]{1,0:T(8,128)(2,1)}, f32[1,32]{1,0:T(1,128)}, f32[1,32]{1,0:T(1,128)}) custom-call(bf16[3,32,3200]{2,1,0:T(8,128)(2,1)S(1)} %get-tuple-element.42.refs_0_, bf16[3,32,3200]{2,1,0:T(8,128)(2,1)S(1)} %collective-permute-done.6.refs_1_, bf16[3,32,3200]{2,1,0:T(8,128)(2,1)S(1)} %collective-permute-done.7.refs_2_, ...), custom_call_target="tpu_custom_call" | custom-call | tf_op jit(solution)/shard_map/last_pass/pallas_call | solution.py:514
  (52 shorter events, 15.3 us)
Async XLA Ops:
  0.7 47.6 %collective-permute-start.1 = (bf16[3136,256]{1,0:T(8,128)(2,1)}, bf16[3136,256]{1,0:T(8,128)(2,1)}, u32[]{:S(2)}, u32[]{:S(2)}) collective-permute-start(bf16[3136,256]{1,0:T(8,128)(2,1)} %bitcast.13), channel_id=1, source_target_pairs={{0,24},{1,7},{2,26},{3,1},{4,28},{5,3},{6,30},{7,5},{8,0},{9,15},{... | collective-permute-start | bytes 4816904 | tf_op jit(solution)/shard_map/ppermute | solution.py:36
  4.3 44.0 %collective-permute-start = (bf16[3136,256]{1,0:T(8,128)(2,1)}, bf16[3136,256]{1,0:T(8,128)(2,1)}, u32[]{:S(2)}, u32[]{:S(2)}) collective-permute-start(bf16[3136,256]{1,0:T(8,128)(2,1)} %bitcast.14), channel_id=1, source_target_pairs={{0,8},{1,3},{2,10},{3,5},{4,12},{5,7},{6,14},{7,1},{8,16},{9,11},{... | collective-permute-start | bytes 4816904 | tf_op jit(solution)/shard_map/ppermute | solution.py:36
  4.3 59.5 %collective-permute-start.13 = (bf16[3136,256]{1,0:T(8,128)(2,1)}, bf16[3136,256]{1,0:T(8,128)(2,1)S(1)}, u32[]{:S(2)}, u32[]{:S(2)}) collective-permute-start(bf16[3136,256]{1,0:T(8,128)(2,1)} %bitcast.15), channel_id=1, source_target_pairs={{0,16},{1,5},{2,18},{3,7},{4,20},{5,1},{6,22},{7,3},{8,24},{9,13},... | collective-permute-start | bytes 4816904 | tf_op jit(solution)/shard_map/ppermute | solution.py:36
  14.1 10.5 %all-to-all-start = ((f32[8,16,128]{2,1,0:T(8,128)}), f32[8,16,128]{2,1,0:T(8,128)S(1)}, u32[]{:S(2)}, u32[]{:S(2)}) async-start(f32[8,16,128]{2,1,0:T(8,128)} %get-tuple-element.40), calls=%async_computation | async-start | bytes 131072 | tf_op jit(solution)/shard_map/all_to_all | solution.py:530
  19.8 14.0 %collective-permute-start.5 = (bf16[64,512]{1,0:T(8,128)(2,1)}, bf16[64,512]{1,0:T(8,128)(2,1)S(1)}, u32[]{:S(2)}, u32[]{:S(2)}) collective-permute-start(bf16[64,512]{1,0:T(8,128)(2,1)} %get-tuple-element.41.refs_7_.refs_5_), channel_id=1, source_target_pairs={{0,2},{1,9},{2,4},{3,11},{4,6},{5,13},{6,0},{7,15},{8,10},{9,17},{... | collective-permute-start | bytes 196616 | tf_op jit(solution)/shard_map/ppermute | solution.py:40
  25.3 23.0 %all-to-all-start.1 = ((f32[16,16,128]{2,1,0:T(8,128)}), f32[16,16,128]{2,1,0:T(8,128)S(1)}, u32[]{:S(2)}, u32[]{:S(2)}) async-start(f32[16,16,128]{2,1,0:T(8,128)} %near_merge.1), calls=%async_computation.1 | async-start | bytes 262144 | tf_op jit(solution)/shard_map/all_to_all | solution.py:530
  30.9 7.1 %collective-permute-start.4 = (bf16[64,512]{1,0:T(8,128)(2,1)}, bf16[64,512]{1,0:T(8,128)(2,1)S(1)}, u32[]{:S(2)}, u32[]{:S(2)}) collective-permute-start(bf16[64,512]{1,0:T(8,128)(2,1)} %get-tuple-element.41.refs_7_.refs_5_), channel_id=1, source_target_pairs={{0,4},{1,17},{2,6},{3,19},{4,0},{5,21},{6,2},{7,23},{8,12},{9,25},... | collective-permute-start | bytes 196616 | tf_op jit(solution)/shard_map/ppermute | solution.py:40
  33.7 8.7 %collective-permute-start.3 = (bf16[64,512]{1,0:T(8,128)(2,1)}, bf16[64,512]{1,0:T(8,128)(2,1)S(1)}, u32[]{:S(2)}, u32[]{:S(2)}) collective-permute-start(bf16[64,512]{1,0:T(8,128)(2,1)} %get-tuple-element.41.refs_7_.refs_5_), channel_id=1, source_target_pairs={{0,6},{1,25},{2,0},{3,27},{4,2},{5,29},{6,4},{7,31},{8,14},{9,1},{... | collective-permute-start | bytes 196616 | tf_op jit(solution)/shard_map/ppermute | solution.py:40
  69.1 4.6 %collective-permute-start.16 = (f32[8,256]{1,0:T(8,128)S(1)}, f32[8,256]{1,0:T(8,128)S(1)}, u32[]{:S(2)}, u32[]{:S(2)}) collective-permute-start(f32[8,256]{1,0:T(8,128)S(1)} %get-tuple-element.51.refs_0_), channel_id=1, source_target_pairs={{0,96},{32,0},{64,32},{96,64},{1,97},{33,1},{65,33},{97,65},{2,98}... | collective-permute-start | bytes 24584 | tf_op jit(solution)/shard_map/ppermute | solution.py:572
  72.9 4.0 %collective-permute-start.15 = (f32[8,256]{1,0:T(8,128)S(1)}, f32[8,256]{1,0:T(8,128)S(1)}, u32[]{:S(2)}, u32[]{:S(2)}) collective-permute-start(f32[8,256]{1,0:T(8,128)S(1)} %get-tuple-element.51.refs_0_), channel_id=1, source_target_pairs={{0,64},{32,96},{64,0},{96,32},{1,65},{33,97},{65,1},{97,33},{2,66}... | collective-permute-start | bytes 24584 | tf_op jit(solution)/shard_map/ppermute | solution.py:572
  77.5 4.3 %collective-permute-start.17 = (bf16[1,32,3200]{2,1,0:T(8,128)(2,1)S(1)}, bf16[1,32,3200]{2,1,0:T(8,128)(2,1)S(1)}, u32[]{:S(2)}, u32[]{:S(2)}) collective-permute-start(bf16[1,32,3200]{2,1,0:T(8,128)(2,1)S(1)} %get-tuple-element.61), channel_id=1, source_target_pairs={{0,1},{1,0},{2,3},{3,2},{4,5},{5,4},{6,7},{7,6},{8,9},{9,8},{10,11... | collective-permute-start | bytes 614408 | tf_op jit(solution)/shard_map/ppermute | solution.py:40
  80.6 27.5 %collective-permute-start.6 = (bf16[3,32,3200]{2,1,0:T(8,128)(2,1)S(1)}, bf16[3,32,3200]{2,1,0:T(8,128)(2,1)S(1)}, u32[]{:S(2)}, u32[]{:S(2)}) collective-permute-start(bf16[3,32,3200]{2,1,0:T(8,128)(2,1)S(1)} %get-tuple-element.43), channel_id=1, source_target_pairs={{0,1},{1,0},{2,3},{3,2},{4,5},{5,4},{6,7},{7,6},{8,9},{9,8},{10,11... | collective-permute-start | bytes 1843208 | tf_op jit(solution)/shard_map/ppermute | solution.py:40
  80.7 30.6 %collective-permute-start.7 = (bf16[3,32,3200]{2,1,0:T(8,128)(2,1)S(1)}, bf16[3,32,3200]{2,1,0:T(8,128)(2,1)S(1)}, u32[]{:S(2)}, u32[]{:S(2)}) collective-permute-start(bf16[3,32,3200]{2,1,0:T(8,128)(2,1)S(1)} %get-tuple-element.44), channel_id=1, source_target_pairs={{0,2},{1,9},{2,4},{3,11},{4,6},{5,13},{6,0},{7,15},{8,10},{9,17},{... | collective-permute-start | bytes 1843208 | tf_op jit(solution)/shard_map/ppermute | solution.py:40
  81.5 11.9 %collective-permute-start.18 = (bf16[1,32,3200]{2,1,0:T(8,128)(2,1)S(1)}, bf16[1,32,3200]{2,1,0:T(8,128)(2,1)S(1)}, u32[]{:S(2)}, u32[]{:S(2)}) collective-permute-start(bf16[1,32,3200]{2,1,0:T(8,128)(2,1)S(1)} %get-tuple-element.62), channel_id=1, source_target_pairs={{0,2},{1,9},{2,4},{3,11},{4,6},{5,13},{6,0},{7,15},{8,10},{9,17},{... | collective-permute-start | bytes 614408 | tf_op jit(solution)/shard_map/ppermute | solution.py:40
  81.5 19.3 %collective-permute-start.19 = (bf16[1,32,3200]{2,1,0:T(8,128)(2,1)S(1)}, bf16[1,32,3200]{2,1,0:T(8,128)(2,1)S(1)}, u32[]{:S(2)}, u32[]{:S(2)}) collective-permute-start(bf16[1,32,3200]{2,1,0:T(8,128)(2,1)S(1)} %get-tuple-element.63), channel_id=1, source_target_pairs={{0,3},{1,8},{2,5},{3,10},{4,7},{5,12},{6,1},{7,14},{8,11},{9,16},{... | collective-permute-start | bytes 614408 | tf_op jit(solution)/shard_map/ppermute | solution.py:40
  81.8 19.1 %collective-permute-start.20 = (bf16[1,32,3200]{2,1,0:T(8,128)(2,1)S(1)}, bf16[1,32,3200]{2,1,0:T(8,128)(2,1)S(1)}, u32[]{:S(2)}, u32[]{:S(2)}) collective-permute-start(bf16[1,32,3200]{2,1,0:T(8,128)(2,1)S(1)} %get-tuple-element.64), channel_id=1, source_target_pairs={{0,4},{1,17},{2,6},{3,19},{4,0},{5,21},{6,2},{7,23},{8,12},{9,25},... | collective-permute-start | bytes 614408 | tf_op jit(solution)/shard_map/ppermute | solution.py:40
  93.4 7.5 %collective-permute-start.21 = (bf16[1,32,3200]{2,1,0:T(8,128)(2,1)S(1)}, bf16[1,32,3200]{2,1,0:T(8,128)(2,1)S(1)}, u32[]{:S(2)}, u32[]{:S(2)}) collective-permute-start(bf16[1,32,3200]{2,1,0:T(8,128)(2,1)S(1)} %get-tuple-element.65), channel_id=1, source_target_pairs={{0,5},{1,16},{2,7},{3,18},{4,1},{5,20},{6,3},{7,22},{8,13},{9,24},... | collective-permute-start | bytes 614408 | tf_op jit(solution)/shard_map/ppermute | solution.py:40
  100.8 4.9 %collective-permute-start.22 = (bf16[1,32,3200]{2,1,0:T(8,128)(2,1)S(1)}, bf16[1,32,3200]{2,1,0:T(8,128)(2,1)S(1)}, u32[]{:S(2)}, u32[]{:S(2)}) collective-permute-start(bf16[1,32,3200]{2,1,0:T(8,128)(2,1)S(1)} %get-tuple-element.66), channel_id=1, source_target_pairs={{0,6},{1,25},{2,0},{3,27},{4,2},{5,29},{6,4},{7,31},{8,14},{9,1},{... | collective-permute-start | bytes 614408 | tf_op jit(solution)/shard_map/ppermute | solution.py:40
  100.8 5.7 %collective-permute-start.23 = (bf16[1,32,3200]{2,1,0:T(8,128)(2,1)S(1)}, bf16[1,32,3200]{2,1,0:T(8,128)(2,1)S(1)}, u32[]{:S(2)}, u32[]{:S(2)}) collective-permute-start(bf16[1,32,3200]{2,1,0:T(8,128)(2,1)S(1)} %get-tuple-element.67), channel_id=1, source_target_pairs={{0,7},{1,24},{2,1},{3,26},{4,3},{5,28},{6,5},{7,30},{8,15},{9,0},{... | collective-permute-start | bytes 614408 | tf_op jit(solution)/shard_map/ppermute | solution.py:40
  100.9 24.0 %collective-permute-start.8 = (bf16[3,32,3200]{2,1,0:T(8,128)(2,1)S(1)}, bf16[3,32,3200]{2,1,0:T(8,128)(2,1)S(1)}, u32[]{:S(2)}, u32[]{:S(2)}) collective-permute-start(bf16[3,32,3200]{2,1,0:T(8,128)(2,1)S(1)} %get-tuple-element.45), channel_id=1, source_target_pairs={{0,3},{1,8},{2,5},{3,10},{4,7},{5,12},{6,1},{7,14},{8,11},{9,16},{... | collective-permute-start | bytes 1843208 | tf_op jit(solution)/shard_map/ppermute | solution.py:40
  105.7 19.2 %collective-permute-start.9 = (bf16[3,32,3200]{2,1,0:T(8,128)(2,1)S(1)}, bf16[3,32,3200]{2,1,0:T(8,128)(2,1)S(1)}, u32[]{:S(2)}, u32[]{:S(2)}) collective-permute-start(bf16[3,32,3200]{2,1,0:T(8,128)(2,1)S(1)} %get-tuple-element.46), channel_id=1, source_target_pairs={{0,4},{1,17},{2,6},{3,19},{4,0},{5,21},{6,2},{7,23},{8,12},{9,25},... | collective-permute-start | bytes 1843208 | tf_op jit(solution)/shard_map/ppermute | solution.py:40
  106.6 18.3 %collective-permute-start.10 = (bf16[3,32,3200]{2,1,0:T(8,128)(2,1)S(1)}, bf16[3,32,3200]{2,1,0:T(8,128)(2,1)S(1)}, u32[]{:S(2)}, u32[]{:S(2)}) collective-permute-start(bf16[3,32,3200]{2,1,0:T(8,128)(2,1)S(1)} %get-tuple-element.47), channel_id=1, source_target_pairs={{0,5},{1,16},{2,7},{3,18},{4,1},{5,20},{6,3},{7,22},{8,13},{9,24},... | collective-permute-start | bytes 1843208 | tf_op jit(solution)/shard_map/ppermute | solution.py:40
  108.1 20.2 %collective-permute-start.11 = (bf16[3,32,3200]{2,1,0:T(8,128)(2,1)S(1)}, bf16[3,32,3200]{2,1,0:T(8,128)(2,1)S(1)}, u32[]{:S(2)}, u32[]{:S(2)}) collective-permute-start(bf16[3,32,3200]{2,1,0:T(8,128)(2,1)S(1)} %get-tuple-element.48), channel_id=1, source_target_pairs={{0,6},{1,25},{2,0},{3,27},{4,2},{5,29},{6,4},{7,31},{8,14},{9,1},{... | collective-permute-start | bytes 1843208 | tf_op jit(solution)/shard_map/ppermute | solution.py:40
  111.3 25.0 %collective-permute-start.12 = (bf16[3,32,3200]{2,1,0:T(8,128)(2,1)S(1)}, bf16[3,32,3200]{2,1,0:T(8,128)(2,1)S(1)}, u32[]{:S(2)}, u32[]{:S(2)}) collective-permute-start(bf16[3,32,3200]{2,1,0:T(8,128)(2,1)S(1)} %get-tuple-element.49), channel_id=1, source_target_pairs={{0,7},{1,24},{2,1},{3,26},{4,3},{5,28},{6,5},{7,30},{8,15},{9,0},{... | collective-permute-start | bytes 1843208 | tf_op jit(solution)/shard_map/ppermute | solution.py:40
  (11 other events, 344.5 us)
